TPU v7x, 32 devices: a whole 2x2x4 slice. The times are simulated.
32 devices in a mesh: gx: 8 (over y, x, core), gy: 4 (over z).
Axes of the slice: x: 2, y: 2, z: 4, core: 2. Of those that a mesh axis runs over, the one named last changes fastest.
Arguments:
- states: bfloat16 [512, 2048], P('gx'), may hold values from -6 to 6
- attn_gain: bfloat16 [2048], replicated, may hold values from 0.099609375 to 1.8984375
- w_qkv: bfloat16 [2048, 5120], P(None, 'gy'), may hold values from -0.125 to 0.125
- q_gain: bfloat16 [128], replicated, may hold values from 0.099609375 to 1.8984375
- k_gain: bfloat16 [128], replicated, may hold values from 0.099609375 to 1.8984375
- cache_k: bfloat16 [8, 4096, 512], P('gx', 'gy'), may hold values from -400 to 400
- cache_v: bfloat16 [8, 4096, 512], P('gx', 'gy'), may hold values from -6 to 6
- cache_len: int32 [8], P('gx'), may hold values from 256 to 4096, as said below
- tree_mask: int32 [8, 64, 64], P('gx'), may hold values from 0 to 1, as said below
- w_o: bfloat16 [4096, 2048], P(None, 'gy'), may hold values from -0.09375 to 0.09375
- ffn_gain: bfloat16 [2048], P('gy'), may hold values from 0.099609375 to 1.8984375
- routing: int32 [512, 8], replicated, may hold values from 0 to 63, all different within a row; in each aligned block of 64 rows (0 to 63, 64 to 127, ...) at most 12 rows name the same one
- route_weight: float32 [512, 8], replicated, may hold values from 0.05 to 0.5
- w_in: bfloat16 [64, 2048, 1536], P('gx', 'gy'), may hold values from -0.125 to 0.125
- w_down: bfloat16 [64, 768, 2048], P('gx', None, 'gy'), may hold values from -0.21875 to 0.21875
- accept: int32 [8, 8, 64], P('gx'), may hold values from 0 to 1, as said below
Outputs:
- layer_out: bfloat16 [512, 2048], P('gx', 'gy')
- accepted_kv: bfloat16 [8, 8, 1024], P('gx')
Inputs may be any that keep to these rules, and one draw needn't show every extreme that they name: `cache_len`: each request's cache holds keys at positions below its length; some request fills all 4096 positions. tree_mask[r, t, u] is 1 exactly when draft token u is t or an ancestor of t in request r's tree; every token's parent has a lower index and token 0 is the root. Row a of accept[r] is the one-hot of the token at depth a on one path from the root of request r's tree; the path is longer than 8 tokens. `routing`: each row names 8 different experts; in each aligned block of 64 rows no expert is named by more than 12 rows.
All inputs are finite; a program needn't handle non-finite values.
Results may differ from a plain program's by a relative error of at most 0.014.
Values may be sent and summed in bfloat16 or wider, within the bound.
A program may use at most 128 MiB of HBM per device.

v0:
```python
import math

import jax
import jax.numpy as jnp
from jax import lax
from jax.sharding import PartitionSpec as P

EPS = 1e-06
NEG = -1e30
THETA_LOG = math.log(1000000.0)


def combined_all(shard, axis, join):
    gathered = jax.tree.map(
        lambda a, kind: lax.all_gather(a.astype(kind), axis),
        shard,
        (jnp.bfloat16, jnp.bfloat16, jnp.bfloat16),
    )

    def take(source):
        return jax.tree.map(
            lambda a, own: lax.dynamic_index_in_dim(a, source, 0, False).astype(own.dtype),
            gathered,
            shard,
        )

    return lax.fori_loop(
        1, lax.axis_size(axis), lambda source, state: join(state, take(source)), take(0)
    )


def rms_scale(values, gain):
    return values * lax.rsqrt(jnp.mean(values * values, -1, keepdims=True) + EPS) * gain


def rotate(values, position):
    half = values.shape[-1] // 2
    freqs = jnp.exp(jnp.arange(half, dtype=jnp.float32) * (-2.0 * THETA_LOG / values.shape[-1]))
    angles = position.astype(jnp.float32)[..., None] * freqs
    cosine = jnp.cos(angles)
    sine = jnp.sin(angles)
    lower = values[..., :half]
    upper = values[..., half:]
    return jnp.concatenate([lower * cosine - upper * sine, upper * cosine + lower * sine], -1)


def combine_parts(earlier, later):
    max_one, sum_one, acc_one = earlier
    max_two, sum_two, acc_two = later
    joined = jnp.maximum(max_one, max_two)
    factor_one = jnp.exp(max_one - joined)
    factor_two = jnp.exp(max_two - joined)
    return (
        joined,
        sum_one * factor_one + sum_two * factor_two,
        acc_one * factor_one[..., None] + acc_two * factor_two[..., None],
    )


def body(
    states,
    attn_gain,
    w_qkv,
    q_gain,
    k_gain,
    cache_k,
    cache_v,
    cache_len,
    tree_mask,
    w_o,
    ffn_gain,
    routing,
    route_weight,
    w_in,
    w_down,
    accept,
):
    tok_rows, model_width = states.shape
    head_dim = q_gain.shape[0]
    kv_cols = cache_k.shape[2]
    kv_heads = kv_cols // head_dim
    heads_all = w_o.shape[0] // head_dim
    group = heads_all // kv_heads
    requests_here, tree_size = (tree_mask.shape[0], tree_mask.shape[1])
    cache_span = cache_k.shape[1]
    cols_here = w_o.shape[1]
    col_index = lax.axis_index("gy")
    row_index = lax.axis_index("gx")
    count_gx = lax.axis_size("gx")
    normed = rms_scale(states.astype(jnp.float32), attn_gain.astype(jnp.float32)).astype(
        jnp.bfloat16
    )
    qkv_part = jnp.dot(normed, w_qkv, preferred_element_type=jnp.float32).astype(jnp.bfloat16)
    qkv_whole = lax.all_gather(qkv_part, "gy", axis=1, tiled=True)
    q_cols = heads_all * head_dim
    query = qkv_whole[:, :q_cols].reshape(requests_here, tree_size, kv_heads, group, head_dim)
    keys_new = qkv_whole[:, q_cols : q_cols + kv_cols].reshape(
        requests_here, tree_size, kv_heads, head_dim
    )
    values_new = qkv_whole[:, q_cols + kv_cols :].reshape(
        requests_here, tree_size, kv_heads, head_dim
    )
    depth = jnp.sum(tree_mask, -1) - 1
    position = cache_len[:, None] + depth
    q_rot = rotate(
        rms_scale(query.astype(jnp.float32), q_gain.astype(jnp.float32)), position[:, :, None, None]
    ).astype(jnp.bfloat16)
    k_rot = rotate(
        rms_scale(keys_new.astype(jnp.float32), k_gain.astype(jnp.float32)), position[:, :, None]
    ).astype(jnp.bfloat16)
    cached_keys = cache_k.reshape(requests_here, cache_span, kv_heads, head_dim)
    cached_values = cache_v.reshape(requests_here, cache_span, kv_heads, head_dim)
    score_scale = head_dim ** (-0.5)
    scores_cache = (
        jnp.einsum("rtkgd,rskd->rtkgs", q_rot, cached_keys, preferred_element_type=jnp.float32)
        * score_scale
    )
    scores_tree = (
        jnp.einsum("rtkgd,rukd->rtkgu", q_rot, k_rot, preferred_element_type=jnp.float32)
        * score_scale
    )
    cache_pos = col_index * cache_span + jnp.arange(cache_span, dtype=jnp.int32)
    valid = (cache_pos[None, :] < cache_len[:, None])[:, None, None, None, :]
    tree_ok = ((tree_mask == 1) & (col_index == 0))[:, :, None, None, :]
    scores_cache = jnp.where(valid, scores_cache, NEG)
    scores_tree = jnp.where(tree_ok, scores_tree, NEG)
    row_max = jnp.maximum(jnp.max(scores_cache, -1), jnp.max(scores_tree, -1))
    probs_cache = jnp.where(valid, jnp.exp(scores_cache - row_max[..., None]), 0.0).astype(
        jnp.bfloat16
    )
    probs_tree = jnp.where(tree_ok, jnp.exp(scores_tree - row_max[..., None]), 0.0).astype(
        jnp.bfloat16
    )
    denom_sum = jnp.sum(probs_cache.astype(jnp.float32), -1) + jnp.sum(
        probs_tree.astype(jnp.float32), -1
    )
    weighted = jnp.einsum(
        "rtkgs,rskd->rtkgd", probs_cache, cached_values, preferred_element_type=jnp.float32
    )
    weighted = weighted + jnp.einsum(
        "rtkgu,rukd->rtkgd", probs_tree, values_new, preferred_element_type=jnp.float32
    )
    row_max, denom_sum, weighted = combined_all((row_max, denom_sum, weighted), "gy", combine_parts)
    attn = (weighted / denom_sum[..., None]).astype(jnp.bfloat16).reshape(tok_rows, q_cols)
    states_here = lax.dynamic_slice_in_dim(states, col_index * cols_here, cols_here, 1)
    resid = (
        states_here.astype(jnp.float32) + jnp.dot(attn, w_o, preferred_element_type=jnp.float32)
    ).astype(jnp.bfloat16)
    exp_here = w_in.shape[0]
    expert_count = exp_here * count_gx
    top_k = routing.shape[1]
    most_rows = 3 * tok_rows * top_k // (2 * expert_count)
    hidden_units = w_down.shape[1]
    gain_float = ffn_gain.astype(jnp.float32)
    own_route = lax.dynamic_slice_in_dim(routing, row_index * tok_rows, tok_rows, 0)
    own_weight = lax.dynamic_slice_in_dim(route_weight, row_index * tok_rows, tok_rows, 0)
    matched = own_route[:, :, None] == jnp.arange(expert_count, dtype=jnp.int32)[None, None, :]
    hit_count = jnp.any(matched, 1).astype(jnp.int32)
    weight_table = jnp.sum(jnp.where(matched, own_weight[:, :, None], 0.0), 1)
    slot_rank = jnp.cumsum(hit_count, 0) - 1
    slot_ids = jnp.where(
        hit_count > 0,
        jnp.arange(expert_count, dtype=jnp.int32)[None, :] * most_rows + slot_rank,
        expert_count * most_rows,
    )
    token_ids = jnp.broadcast_to(jnp.arange(tok_rows, dtype=jnp.int32)[:, None], slot_ids.shape)
    slot_table = (
        jnp.full((expert_count * most_rows,), tok_rows, jnp.int32)
        .at[slot_ids]
        .set(token_ids, mode="drop")
    )
    padded = jnp.concatenate([resid, jnp.zeros((1, cols_here), jnp.bfloat16)], 0)
    outgoing = padded[slot_table].reshape(expert_count, most_rows, cols_here)
    arrived = lax.all_to_all(outgoing, "gx", split_axis=0, concat_axis=1, tiled=True)
    arrived_float = arrived.astype(jnp.float32)
    squares = jnp.sum(arrived_float * arrived_float, -1)
    scaled = (arrived_float * gain_float).astype(jnp.bfloat16)
    partial_value = jnp.einsum("esd,edf->esf", scaled, w_in, preferred_element_type=jnp.float32)
    summed, squares = (
        lax.psum_scatter(
            partial_value.astype(jnp.bfloat16), "gy", scatter_dimension=1, tiled=True
        ).astype(jnp.float32),
        lax.psum_scatter(
            squares.astype(jnp.bfloat16), "gy", scatter_dimension=1, tiled=True
        ).astype(jnp.float32),
    )
    inverse = lax.rsqrt(squares / model_width + EPS)[..., None]
    hidden = (
        jax.nn.silu(summed[..., :hidden_units] * inverse) * (summed[..., hidden_units:] * inverse)
    ).astype(jnp.bfloat16)
    expert_out = jnp.einsum(
        "esf,efd->esd",
        lax.all_gather(hidden, "gy", axis=1, tiled=True),
        w_down,
        preferred_element_type=jnp.float32,
    )
    returned = lax.all_to_all(
        expert_out.astype(jnp.bfloat16), "gx", split_axis=1, concat_axis=0, tiled=True
    ).astype(expert_out.dtype)
    weight_pad = jnp.concatenate([weight_table, jnp.zeros((1, expert_count), jnp.float32)], 0)
    slot_expert = jnp.arange(expert_count * most_rows, dtype=jnp.int32) // most_rows
    slot_weight = weight_pad[slot_table, slot_expert]
    moe_total = (
        jnp.zeros((tok_rows + 1, cols_here), jnp.float32)
        .at[slot_table]
        .add(returned.reshape(-1, cols_here) * slot_weight[:, None])[:tok_rows]
    )
    layer_out = (resid.astype(jnp.float32) + moe_total).astype(jnp.bfloat16)
    kv_new = jnp.concatenate(
        [
            k_rot.reshape(requests_here, tree_size, kv_cols),
            values_new.reshape(requests_here, tree_size, kv_cols),
        ],
        -1,
    )
    accepted_kv = jnp.einsum(
        "rat,rtc->rac", accept.astype(jnp.bfloat16), kv_new, preferred_element_type=jnp.float32
    ).astype(jnp.bfloat16)
    return (layer_out, accepted_kv)


def solution(mesh):
    in_specs = (
        P("gx", None),
        P(),
        P(None, "gy"),
        P(),
        P(),
        P("gx", "gy", None),
        P("gx", "gy", None),
        P("gx"),
        P("gx", None, None),
        P(None, "gy"),
        P("gy"),
        P(),
        P(),
        P("gx", "gy", None),
        P("gx", None, "gy"),
        P("gx", None, None),
    )
    out_specs = (P("gx", "gy"), P("gx", None, None))
    return jax.shard_map(body, mesh=mesh, in_specs=in_specs, out_specs=out_specs, check_vma=False)
```

profile of v0, /device:TPU:1, one launch (start us, length us, event | category | flops | bytes accessed | tf_op | source)
XLA Modules:
  0.0 281.5 jit_solution(2547359270046433330)
XLA Ops:
  9.1 3.7 %convolution_convert_fusion.1 = bf16[64,1280]{1,0:T(8,128)(2,1)S(1)} fusion(bf16[2048,1280]{1,0:T(8,128)(2,1)} %param.20, bf16[64,2048]{1,0:T(8,128)(2,1)} %param.18, f32[2048]{0:T(1024)S(1)} %convert_element_type.348, f32[64]{0:T(128)S(1)} %add_rsqrt_fusion.3), kind=kOutput, calls=%fused_computation.23 | convolution fusion | flops 336150528 | bytes 5677312 | tf_op jit(solution)/shard_map/dot_general | solution.py:93
  12.7 16.2 %all_gather.20 = bf16[64,5120]{1,0:T(8,128)(2,1)S(1)} all-gather(bf16[64,1280]{1,0:T(8,128)(2,1)S(1)} %convolution_convert_fusion.1), channel_id=1, replica_groups=mesh['gx'=8,'gy'=4] {'gy'}, dimensions={1}, use_global_device_ids=true | all-gather | bytes 819200 | tf_op jit(solution)/shard_map/all_gather | solution.py:94
  33.0 4.7 %fusion.6 = (f32[64,4,8]{2,0,1:T(8,128)S(1)}, f32[4,64,8,1024]{3,2,1,0:T(8,128)}) fusion(pred[1024]{0:T(1024)(128)(4,1)S(1)} %add_compare_fusion, bf16[64,4,8,128]{3,2,0,1:T(8,128)(2,1)S(1)} %pad_maximum_fusion, bf16[1024,4,128,1]{2,1,0,3:T(4,128)(2,1)S(1)} %bitcast.184), kind=kOutput, calls=%fused_computation.18 | convolution fusion | flops 543160320 | bytes 9970688 | tf_op jit(solution)/shard_map/rtkgd,rskd->rtkgs/dot_general | solution.py:115
  40.5 5.5 %fusion.24 = bf16[1,64,4,8,128]{4,3,1,2,0:T(8,128)(2,1)S(1)} fusion(f32[4,128,64,8]{1,3,2,0:T(8,128)S(1)} %fusion.56, bf16[1024,4,128,1]{2,1,0,3:T(4,128)(2,1)S(1)} %bitcast.189, f32[4,64,8,1024]{3,2,1,0:T(8,128)} %get-tuple-element.264, f32[64,4,8]{2,0,1:T(8,128)S(1)} %copy.215, pred[1024]{0:T(1024)(128)(4,1)S(1)} %add_compare_fusion), kind=kOutput, calls=%fused_computation.38 | convolution fusion | flops 547880960 | bytes 11019264 | tf_op jit(solution)/shard_map/rtkgs,rskd->rtkgd/dot_general | solution.py:137
  48.0 15.4 %fusion.77 = s32[64,64,1]{2,1,0:T(8,128)S(1)} fusion(s32[64,64,1]{2,1,0:T(8,128)S(1)} %copy.232), kind=kOutput, calls=%fused_computation.141 | output fusion | flops 258048 | bytes 32768 | tf_op jit(solution)/shard_map/jit(cumsum)/reduce_window_sum | solution.py:160
  63.4 1.2 fusion.9
  65.0 13.2 %all-gather = bf16[256,4,8]{2,1,0:T(4,128)(2,1)S(1)} all-gather(bf16[64,4,8]{2,1,0:T(4,128)(2,1)S(1)} %copy.214), channel_id=2, replica_groups=mesh['gx'=8,'gy'=4] {'gy'}, dimensions={0}, use_global_device_ids=true | all-gather | bytes 20480 | tf_op jit(solution)/shard_map/all_gather | solution.py:15
  78.3 4.7 %convert_reduce_fusion = f32[64,4,8]{2,0,1:T(8,128)S(1)} fusion(f32[64,4,8]{2,0,1:T(8,128)S(1)} %copy.215, f32[4,64,8,1024]{3,2,1,0:T(8,128)} %get-tuple-element.264, pred[1024]{0:T(1024)(128)(4,1)S(1)} %add_compare_fusion), kind=kLoop, calls=%fused_computation.16 | loop fusion | flops 14678016 | bytes 8406016 | tf_op jit(solution)/shard_map/reduce_sum | solution.py:134
  83.2 13.6 %all-gather.1 = bf16[256,4,8]{2,1,0:T(4,128)(2,1)S(1)} all-gather(bf16[64,4,8]{2,1,0:T(4,128)(2,1)S(1)} %copy.217), channel_id=3, replica_groups=mesh['gx'=8,'gy'=4] {'gy'}, dimensions={0}, use_global_device_ids=true | all-gather | bytes 20480 | tf_op jit(solution)/shard_map/all_gather | solution.py:15
  97.3 15.5 %scatter_custom_fusion = s32[768]{0:T(1024)S(1)} fusion(s32[4096]{0:T(1024)S(1)} %reshape.728, s32[4096]{0:T(1024)S(1)} %reshape.730, s32[]{:T(128)} %constant.123.clone.1), kind=kCustom, calls=%fused_computation.123 | custom fusion | bytes 3076 | tf_op jit(solution)/shard_map/scatter | solution.py:170
  112.8 1.2 slice_convert_fusion
  114.0 6.7 %while.19 = (s32[]{:T(128)}, f32[1,64,4,8]{1,3,2,0:T(8,128)S(1)}, f32[1,64,4,8]{1,3,2,0:T(8,128)S(1)}, f32[1,64,4,8,128]{4,3,2,1,0:T(8,128)S(1)}, bf16[4,1,64,4,...) while((s32[]{:T(128)}, f32[1,64,4,8]{1,3,2,0:T(8,128)S(1)}, ...), condition=%wide.region_9.10_spmd, body=%wide.region_8.9_spmd.sunk | while | flops 1069061 | bytes 2764955 | solution.py:27
  114.3 1.9 fusion.92
  116.6 1.9 fusion.92
  118.8 1.9 fusion.92
  121.5 3.0 %fusion.27 = bf16[64,512]{1,0:T(8,128)(2,1)S(1)} fusion(bf16[64,4096]{1,0:T(8,128)(2,1)S(1)} %reshape.695, bf16[4096,512]{1,0:T(8,128)(2,1)} %param.27, bf16[64,2048]{1,0:T(8,128)(2,1)} %param.18, s32[]{:T(128)S(6)} %select_n.93), kind=kOutput, calls=%fused_computation.40 | convolution fusion | flops 268533760 | bytes 4849668 | tf_op jit(solution)/shard_map/dot_general | solution.py:147
  124.5 2.7 gather_fusion
  128.4 12.2 %all-to-all-start = ((bf16[64,12,512]{2,1,0:T(8,128)(2,1)}), bf16[64,12,512]{2,1,0:T(8,128)(2,1)S(1)}, u32[]{:S(2)}, u32[]{:S(2)}) async-start(bf16[64,12,512]{2,1,0:T(8,128)(2,1)} %reshape.696), calls=%async_computation | async-start | bytes 2097152 | tf_op jit(solution)/shard_map/all_to_all | solution.py:174
  140.6 11.9 %all-to-all-done = bf16[64,12,512]{2,1,0:T(8,128)(2,1)S(1)} async-done(((bf16[64,12,512]{2,1,0:T(8,128)(2,1)}), bf16[64,12,512]{2,1,0:T(8,128)(2,1)S(1)}, u32[]{:S(2)}, u32[]{:S(2)}) %all-to-all-start) | async-done | bytes 786464 | tf_op jit(solution)/shard_map/all_to_all | solution.py:174
  153.2 6.7 %fusion.74 = bf16[12,8,8,1536]{3,1,0,2:T(8,128)(2,1)S(1)} fusion(bf16[8,512,1536]{2,1,0:T(8,128)(2,1)} %param.31, bf16[8,96,512]{2,0,1:T(8,128)(2,1)S(1)} %fusion.10), kind=kOutput, calls=%fused_computation.140 | convolution fusion | flops 1209139200 | bytes 15728640 | tf_op jit(solution)/shard_map/esd,edf->esf/dot_general | solution.py:178
  159.9 1.7 copy.265
  164.2 9.3 %all-reduce.2 = bf16[8,96]{1,0:T(8,128)(2,1)S(1)} all-reduce(bf16[8,96]{1,0:T(8,128)(2,1)S(1)} %convert_element_type.390), channel_id=6, replica_groups=mesh['gx'=8,'gy'=4] {'gy'}, use_global_device_ids=true, to_apply=%region_15.16.clone | all-reduce | flops 768 | bytes 3072
  173.5 37.6 %reduce-scatter.5.cloned.1.call-done = bf16[24,12288]{1,0:T(8,128)(2,1)} async-done(((bf16[96,12288]{1,0:T(8,128)(2,1)}), bf16[24,12288]{1,0:T(8,128)(2,1)}) %reduce-scatter.5.cloned.1.call-update) | async-done | bytes 589840
  211.2 1.2 copy.266
  213.6 29.6 %all-gather.6.cloned.1.call-done = bf16[8,96,768]{2,1,0:T(8,128)(2,1)} async-done(((bf16[8,24,768]{2,1,0:T(8,128)(2,1)}), bf16[8,96,768]{2,1,0:T(8,128)(2,1)}) %all-gather.6.cloned.1.call-update) | async-done | bytes 1179664 | tf_op jit(solution)/shard_map/all_gather | solution.py:193
  243.2 4.3 %convolution_convert_fusion.2 = bf16[8,96,512]{2,1,0:T(8,128)(2,1)S(1)} fusion(bf16[8,96,768]{2,1,0:T(8,128)(2,1)} %all-gather.6.cloned.1.call-done, bf16[8,768,512]{2,1,0:T(8,128)(2,1)} %param.32), kind=kOutput, calls=%fused_computation.31 | convolution fusion | flops 604372992 | bytes 8257536 | tf_op jit(solution)/shard_map/esf,efd->esd/dot_general | solution.py:191
  247.5 1.3 copy.238
  248.8 4.9 %all-to-all-start.1 = ((bf16[8,96,512]{2,0,1:T(8,128)(2,1)}), bf16[8,96,512]{2,0,1:T(8,128)(2,1)S(1)}, u32[]{:S(2)}, u32[]{:S(2)}) async-start(bf16[8,96,512]{2,0,1:T(8,128)(2,1)} %copy.238), calls=%async_computation.1 | async-start | bytes 1572864 | tf_op jit(solution)/shard_map/all_to_all | solution.py:197
  254.9 5.1 %gather_fusion.1 = f32[768]{0:T(1024)S(1)} fusion(f32[65,64]{1,0:T(8,128)S(1)} %concatenate.45, s32[768]{0:T(1024)S(1)} %fusion.62), kind=kCustom, calls=%fused_computation.1 | custom fusion | bytes 12288 | tf_op jit(solution)/shard_map/gather | solution.py:202
  260.9 1.9 all-to-all-done.1
  264.0 1.3 reshape.709
  265.3 9.0 %scatter_custom_fusion.1 = f32[65,512]{1,0:T(8,128)S(1)} fusion(s32[768]{0:T(1024)S(1)} %get-tuple-element.260, f32[768,512]{1,0:T(8,128)} %reshape.709, f32[768]{0:T(1024)S(1)} %gather_fusion.1, f32[]{:T(128)} %constant.113.clone.1), kind=kCustom, calls=%fused_computation.29 | custom fusion | flops 786432 | bytes 1710084 | tf_op jit(solution)/shard_map/scatter-add | solution.py:206
  (131 shorter events, 21.0 us)
Async XLA Ops:
  7.2 39.8 %copy-start = (s32[512,8]{0,1:T(8,128)S(1)}, s32[512,8]{0,1:T(8,128)}, u32[]{:S(2)}) copy-start(s32[512,8]{0,1:T(8,128)} %param.29) | copy-start | bytes 49156
  7.2 105.7 %all-gather.8.cloned.1.call-start = ((), (), s32[]{:S(2)}) async-start(), calls=%async_computation.4 | async-start | bytes 2621440 | tf_op jit(solution)/shard_map/all_gather | solution.py:15
  12.7 17.9 %copy-start.8 = (bf16[128]{0:T(256)(128)(2,1)S(1)}, bf16[128]{0:T(256)(128)(2,1)}, u32[]{:S(2)}) copy-start(bf16[128]{0:T(256)(128)(2,1)} %param.21) | copy-start | bytes 772
  29.1 2.2 copy-start.4
  29.1 2.3 copy-start.2
  33.0 4.8 %copy-start.9 = (bf16[128]{0:T(256)(128)(2,1)S(1)}, bf16[128]{0:T(256)(128)(2,1)}, u32[]{:S(2)}) copy-start(bf16[128]{0:T(256)(128)(2,1)} %param.22) | copy-start | bytes 772
  38.4 1.4 copy-start.3
  127.2 13.3 %copy-start.6 = (bf16[512]{0:T(512)(128)(2,1)S(1)}, bf16[512]{0:T(512)(128)(2,1)}, u32[]{:S(2)}) copy-start(bf16[512]{0:T(512)(128)(2,1)} %param.28) | copy-start | bytes 3076
  128.4 24.1 %all-to-all-start = ((bf16[64,12,512]{2,1,0:T(8,128)(2,1)}), bf16[64,12,512]{2,1,0:T(8,128)(2,1)S(1)}, u32[]{:S(2)}, u32[]{:S(2)}) async-start(bf16[64,12,512]{2,1,0:T(8,128)(2,1)} %reshape.696), calls=%async_computation | async-start | bytes 2097152 | tf_op jit(solution)/shard_map/all_to_all | solution.py:174
  140.5 70.6 %reduce-scatter.5.cloned.1.call-start = ((), (), s32[]{:S(2)}) async-start(), calls=%async_computation.5 | async-start | bytes 2949120
  161.6 0.7 copy-start.10
  161.6 81.6 %all-gather.6.cloned.1.call-start = ((), (), s32[]{:S(2)}) async-start(), calls=%async_computation.3 | async-start | bytes 1474560 | tf_op jit(solution)/shard_map/all_gather | solution.py:193
  248.8 14.0 %all-to-all-start.1 = ((bf16[8,96,512]{2,0,1:T(8,128)(2,1)}), bf16[8,96,512]{2,0,1:T(8,128)(2,1)S(1)}, u32[]{:S(2)}, u32[]{:S(2)}) async-start(bf16[8,96,512]{2,0,1:T(8,128)(2,1)} %copy.238), calls=%async_computation.1 | async-start | bytes 1572864 | tf_op jit(solution)/shard_map/all_to_all | solution.py:197
  254.8 5.3 %copy-start.5 = (bf16[1,64,512]{2,1,0:T(8,128)(2,1)S(1)}, bf16[1,64,512]{2,1,0:T(8,128)(2,1)}, u32[]{:S(2)}) copy-start(bf16[1,64,512]{2,1,0:T(8,128)(2,1)} %get-tuple-element.254) | copy-start | bytes 196612
  254.9 5.3 %copy-start.7 = (s32[1,8,64]{2,1,0:T(8,128)S(1)}, s32[1,8,64]{2,1,0:T(8,128)}, u32[]{:S(2)}) copy-start(s32[1,8,64]{2,1,0:T(8,128)} %param.33) | copy-start | bytes 6148
  263.0 11.9 %copy-start.1 = (s32[512,8]{0,1:T(8,128)S(1)}, s32[512,8]{0,1:T(8,128)}, u32[]{:S(2)}) copy-start(s32[512,8]{0,1:T(8,128)} %param.29) | copy-start | bytes 49156
Sparse Core Ops, SparseCore 0:
  47.0 56.6 all-gather.7
  161.7 49.3 reduce-scatter.4
  213.7 29.4 all-gather.5
where the time goes:
time: 286 us; the launch traced here: 281 us
  waiting for transfers between devices  81.2 us (28%)
  blocking collectives  52.4 us (18%)
  other arithmetic  46 us (16%)
  local copies, waits for them, and re-layouts  39.4 us (14%)
  matrix products  29.6 us (10%)
  starting transfers between devices  17.2 us (6%)
  between operations  15.7 us (5%)
    unnamed x4, waiting for transfers between devices  37.7 us
    all_gather x1, waiting for transfers between devices, body(): lax.all_gather(hidden, 'gy', axis=1, tiled=True)  29.6 us
    all_gather x2, blocking collectives, combined_all(): lax.all_gather(a.astype(kind), axis)  26.8 us
    all_gather x1, blocking collectives, body(): qkv_whole = lax.all_gather(qkv_part, 'gy', axis=1, tiled=True)  16.2 us
    scatter x1, local copies, waits for them, and re-layouts, body(): slot_table = jnp.full((expert_count * most_rows,), tok_rows, jnp.int32).a...  15.5 us
    another operation x1, other arithmetic, body(): slot_rank = jnp.cumsum(hit_count, 0) - 1  15.4 us
    all_to_all x1, starting transfers between devices, body(): lax.all_to_all(outgoing, 'gx', split_axis=0, concat_axis=1, tiled=True)  12.2 us
    all_to_all x1, waiting for transfers between devices, body(): lax.all_to_all(outgoing, 'gx', split_axis=0, concat_axis=1, tiled=True)  11.9 us
  transfers between devices with their start and end apart: 5, of which 4 were waited for; matrix products, arithmetic and copies ran while one was open for 17% of the time, Pallas kernels for 0%

commit v1 on v0

v1 whole, which is shorter than its diff:
```python
import math

import jax
import jax.numpy as jnp
from jax import lax
from jax.experimental import pallas as pl
from jax.experimental.pallas import tpu as pltpu
from jax.sharding import PartitionSpec as P

EPS = 1e-06
NEG = -1e30
THETA_LOG = math.log(1000000.0)


MESH = pl.DeviceIdType.MESH


def exchange(arrays, axis, scatter, cid):
    count = lax.axis_size(axis)
    number = len(arrays)

    def kernel(*refs):
        ins, outs = refs[:number], refs[number : 2 * number]
        send, recv, local = refs[2 * number :]
        me = lax.axis_index(axis)
        barrier = pltpu.get_barrier_semaphore()
        for d in range(1, count):
            pl.semaphore_signal(
                barrier, inc=1, device_id={axis: lax.rem(me + d, count)}, device_id_type=MESH
            )
        pl.semaphore_wait(barrier, count - 1)
        copies = []
        for d in range(1, count):
            peer = lax.rem(me + d, count)
            for i in range(number):
                copy = pltpu.make_async_remote_copy(
                    src_ref=ins[i].at[peer] if scatter else ins[i],
                    dst_ref=outs[i].at[me],
                    send_sem=send.at[i, d],
                    recv_sem=recv.at[i, d],
                    device_id={axis: peer},
                    device_id_type=MESH,
                )
                copy.start()
                copies.append(copy)
        own = []
        for i in range(number):
            copy = pltpu.make_async_copy(
                ins[i].at[me] if scatter else ins[i], outs[i].at[me], local.at[i]
            )
            copy.start()
            own.append(copy)
        for copy in own + copies:
            copy.wait()

    outs = [
        jax.ShapeDtypeStruct(x.shape if scatter else (count,) + x.shape, x.dtype) for x in arrays
    ]
    return pl.pallas_call(
        kernel,
        out_shape=outs,
        in_specs=[pl.BlockSpec(memory_space=pltpu.VMEM)] * number,
        out_specs=[pl.BlockSpec(memory_space=pltpu.VMEM)] * number,
        scratch_shapes=[
            pltpu.SemaphoreType.DMA((number, count)),
            pltpu.SemaphoreType.DMA((number, count)),
            pltpu.SemaphoreType.DMA((number,)),
        ],
        compiler_params=pltpu.CompilerParams(collective_id=cid, has_side_effects=True),
        name="exchange_%d" % cid,
    )(*arrays)


def expert_hidden(rows, squares, w_in, model_width, cid):
    axis = "gy"
    count = lax.axis_size(axis)
    experts, slots, depth = rows.shape
    wide = w_in.shape[2]
    units = wide // 2
    half = experts // 2
    sub = 2
    piece = slots // sub
    chunks = half * sub
    lag = 2

    def kernel(
        x_ref, sq_ref, w_hbm, hid_ref, wbuf, part, rbuf, sqbuf, inv_ref,
        wsem, rs_s, rs_r, h_s, h_r, sq_s, sq_r,
    ):
        me = lax.axis_index(axis)
        prev = lax.rem(me + count - 1, count)
        nxt = lax.rem(me + 1, count)
        at_low = me == 0
        at_high = me == count - 1

        def load(e):
            return pltpu.make_async_copy(w_hbm.at[e], wbuf.at[e], wsem.at[e])

        for s in range(half):
            load(half + s).start()
            load(s).start()
        barrier = pltpu.get_barrier_semaphore()
        for d in range(1, count):
            pl.semaphore_signal(
                barrier, inc=1, device_id={axis: lax.rem(me + d, count)}, device_id_type=MESH
            )
        pl.semaphore_wait(barrier, count - 1)

        def sq_copy(d):
            return pltpu.make_async_remote_copy(
                src_ref=sq_ref,
                dst_ref=sqbuf.at[d],
                send_sem=sq_s.at[d],
                recv_sem=sq_r.at[d],
                device_id={axis: lax.rem(me + d, count)},
                device_id_type=MESH,
            )

        for d in range(1, count):
            sq_copy(d).start()
        total = sq_ref[...]
        for d in range(1, count):
            sq_copy(d).wait()
            total = total + sqbuf[d]
        inv_ref[...] = lax.rsqrt(total / model_width + EPS)
        diagonal = lax.broadcasted_iota(jnp.int32, (piece, 128), 0) == lax.broadcasted_iota(
            jnp.int32, (piece, 128), 1
        )

        def rs_copy(h, c):
            return pltpu.make_async_remote_copy(
                src_ref=part.at[h, c],
                dst_ref=rbuf.at[h, c],
                send_sem=rs_s.at[h, c],
                recv_sem=rs_r.at[h, c],
                device_id={axis: nxt if h else prev},
                device_id_type=MESH,
            )

        def hid_copy(h, c):
            return pltpu.make_async_remote_copy(
                src_ref=hid_ref.at[h, c],
                dst_ref=hid_ref.at[h, c],
                send_sem=h_s.at[h, c],
                recv_sem=h_r.at[h, c],
                device_id={axis: prev if h else nxt},
                device_id_type=MESH,
            )

        def ends(h):
            return (at_low, at_high) if h else (at_high, at_low)

        def reduce_chunk(h, c):
            first, last = ends(h)

            @pl.when(jnp.logical_not(first))
            def _():
                rs_copy(h, c).wait_recv()

            @pl.when(jnp.logical_not(jnp.logical_or(first, last)))
            def _():
                part[h, c] = (
                    part[h, c].astype(jnp.float32) + rbuf[h, c].astype(jnp.float32)
                ).astype(jnp.bfloat16)

            @pl.when(jnp.logical_not(last))
            def _():
                rs_copy(h, c).start()

            @pl.when(last)
            def _():
                row = inv_ref[pl.ds(h * chunks + c, 1), :]
                inverse = jnp.sum(jnp.where(diagonal, row, 0.0), 1, keepdims=True)
                summed = part[h, c].astype(jnp.float32) + rbuf[h, c].astype(jnp.float32)
                gate = summed[:, :units] * inverse
                up = summed[:, units:] * inverse
                hid_ref[h, c] = (gate / (1.0 + jnp.exp(-gate)) * up).astype(jnp.bfloat16)
                hid_copy(h, c).start()

        def return_chunk(h, c):
            first, last = ends(h)

            @pl.when(jnp.logical_not(last))
            def _():
                hid_copy(h, c).wait_recv()

            @pl.when(jnp.logical_not(jnp.logical_or(first, last)))
            def _():
                hid_copy(h, c).start()

        def step(s, carry):
            @pl.when(s < half)
            def _():
                for h in (1, 0):
                    e = h * half + s
                    load(e).wait()
                    value = jnp.dot(x_ref[e], wbuf[e], preferred_element_type=jnp.float32)
                    for j in range(sub):
                        part[h, s * sub + j] = value[j * piece : (j + 1) * piece].astype(
                            jnp.bfloat16
                        )
                for j in range(sub):
                    for h in (1, 0):
                        reduce_chunk(h, s * sub + j)

            @pl.when(s >= lag)
            def _():
                for j in range(sub):
                    for h in (1, 0):
                        return_chunk(h, (s - lag) * sub + j)

            return carry

        lax.fori_loop(0, half + lag, step, 0)

        def finish(c, carry):
            for h in (1, 0):
                first, last = ends(h)

                @pl.when(jnp.logical_not(last))
                def _():
                    rs_copy(h, c).wait_send()

                @pl.when(jnp.logical_not(first))
                def _():
                    hid_copy(h, c).wait_send()

            return carry

        lax.fori_loop(0, chunks, finish, 0)

    hidden = pl.pallas_call(
        kernel,
        out_shape=jax.ShapeDtypeStruct((2, chunks, piece, units), jnp.bfloat16),
        in_specs=[
            pl.BlockSpec(memory_space=pltpu.VMEM),
            pl.BlockSpec(memory_space=pltpu.VMEM),
            pl.BlockSpec(memory_space=pl.ANY),
        ],
        out_specs=pl.BlockSpec(memory_space=pltpu.VMEM),
        scratch_shapes=[
            pltpu.VMEM((experts, depth, wide), jnp.bfloat16),
            pltpu.VMEM((2, chunks, piece, wide), jnp.bfloat16),
            pltpu.VMEM((2, chunks, piece, wide), jnp.bfloat16),
            pltpu.VMEM((count, 2 * chunks, 128), jnp.float32),
            pltpu.VMEM((2 * chunks, 128), jnp.float32),
            pltpu.SemaphoreType.DMA((experts,)),
            pltpu.SemaphoreType.DMA((2, chunks)),
            pltpu.SemaphoreType.DMA((2, chunks)),
            pltpu.SemaphoreType.DMA((2, chunks)),
            pltpu.SemaphoreType.DMA((2, chunks)),
            pltpu.SemaphoreType.DMA((count,)),
            pltpu.SemaphoreType.DMA((count,)),
        ],
        compiler_params=pltpu.CompilerParams(
            collective_id=cid, has_side_effects=True, vmem_limit_bytes=48 * 1024 * 1024
        ),
        name="expert_hidden",
    )(rows, squares, w_in)
    return hidden.reshape(experts, slots, units)


def rms_scale(values, gain):
    return values * lax.rsqrt(jnp.mean(values * values, -1, keepdims=True) + EPS) * gain


def rotate(values, position):
    half = values.shape[-1] // 2
    freqs = jnp.exp(jnp.arange(half, dtype=jnp.float32) * (-2.0 * THETA_LOG / values.shape[-1]))
    angles = position.astype(jnp.float32)[..., None] * freqs
    cosine = jnp.cos(angles)
    sine = jnp.sin(angles)
    lower = values[..., :half]
    upper = values[..., half:]
    return jnp.concatenate([lower * cosine - upper * sine, upper * cosine + lower * sine], -1)


def body(
    states,
    attn_gain,
    w_qkv,
    q_gain,
    k_gain,
    cache_k,
    cache_v,
    cache_len,
    tree_mask,
    w_o,
    ffn_gain,
    routing,
    route_weight,
    w_in,
    w_down,
    accept,
):
    tok_rows, model_width = states.shape
    head_dim = q_gain.shape[0]
    kv_cols = cache_k.shape[2]
    kv_heads = kv_cols // head_dim
    heads_all = w_o.shape[0] // head_dim
    group = heads_all // kv_heads
    requests_here, tree_size = (tree_mask.shape[0], tree_mask.shape[1])
    cache_span = cache_k.shape[1]
    cols_here = w_o.shape[1]
    col_index = lax.axis_index("gy")
    row_index = lax.axis_index("gx")
    count_gx = lax.axis_size("gx")
    normed = rms_scale(states.astype(jnp.float32), attn_gain.astype(jnp.float32)).astype(
        jnp.bfloat16
    )
    qkv_part = jnp.dot(normed, w_qkv, preferred_element_type=jnp.float32).astype(jnp.bfloat16)
    (qkv_blocks,) = exchange([qkv_part], "gy", False, 0)
    qkv_whole = jnp.swapaxes(qkv_blocks, 0, 1).reshape(tok_rows, -1)
    q_cols = heads_all * head_dim
    query = qkv_whole[:, :q_cols].reshape(requests_here, tree_size, kv_heads, group, head_dim)
    keys_new = qkv_whole[:, q_cols : q_cols + kv_cols].reshape(
        requests_here, tree_size, kv_heads, head_dim
    )
    values_new = qkv_whole[:, q_cols + kv_cols :].reshape(
        requests_here, tree_size, kv_heads, head_dim
    )
    depth = jnp.sum(tree_mask, -1) - 1
    position = cache_len[:, None] + depth
    q_rot = rotate(
        rms_scale(query.astype(jnp.float32), q_gain.astype(jnp.float32)), position[:, :, None, None]
    ).astype(jnp.bfloat16)
    k_rot = rotate(
        rms_scale(keys_new.astype(jnp.float32), k_gain.astype(jnp.float32)), position[:, :, None]
    ).astype(jnp.bfloat16)
    cached_keys = cache_k.reshape(requests_here, cache_span, kv_heads, head_dim)
    cached_values = cache_v.reshape(requests_here, cache_span, kv_heads, head_dim)
    score_scale = head_dim ** (-0.5)
    scores_cache = (
        jnp.einsum("rtkgd,rskd->rtkgs", q_rot, cached_keys, preferred_element_type=jnp.float32)
        * score_scale
    )
    scores_tree = (
        jnp.einsum("rtkgd,rukd->rtkgu", q_rot, k_rot, preferred_element_type=jnp.float32)
        * score_scale
    )
    cache_pos = col_index * cache_span + jnp.arange(cache_span, dtype=jnp.int32)
    valid = (cache_pos[None, :] < cache_len[:, None])[:, None, None, None, :]
    tree_ok = ((tree_mask == 1) & (col_index == 0))[:, :, None, None, :]
    scores_cache = jnp.where(valid, scores_cache, NEG)
    scores_tree = jnp.where(tree_ok, scores_tree, NEG)
    row_max = jnp.maximum(jnp.max(scores_cache, -1), jnp.max(scores_tree, -1))
    probs_cache = jnp.where(valid, jnp.exp(scores_cache - row_max[..., None]), 0.0).astype(
        jnp.bfloat16
    )
    probs_tree = jnp.where(tree_ok, jnp.exp(scores_tree - row_max[..., None]), 0.0).astype(
        jnp.bfloat16
    )
    denom_sum = jnp.sum(probs_cache.astype(jnp.float32), -1) + jnp.sum(
        probs_tree.astype(jnp.float32), -1
    )
    weighted = jnp.einsum(
        "rtkgs,rskd->rtkgd", probs_cache, cached_values, preferred_element_type=jnp.float32
    )
    weighted = weighted + jnp.einsum(
        "rtkgu,rukd->rtkgd", probs_tree, values_new, preferred_element_type=jnp.float32
    )
    count_gy = lax.axis_size("gy")
    heads_here = heads_all // count_gy
    blocks = jnp.swapaxes(
        weighted.astype(jnp.bfloat16).reshape(tok_rows, count_gy, heads_here * head_dim), 0, 1
    )
    stats = jnp.stack([row_max, denom_sum]).reshape(2, tok_rows, count_gy, heads_here)
    stats = stats.transpose(2, 0, 1, 3).reshape(count_gy, -1, 128)
    blocks, stats = exchange([blocks, stats], "gy", True, 1)
    stats = stats.reshape(count_gy, 2, tok_rows, heads_here)
    factor = jnp.exp(stats[:, 0] - jnp.max(stats[:, 0], 0))
    denom = jnp.sum(stats[:, 1] * factor, 0)
    factor = factor / denom
    attn_part = jnp.sum(
        blocks.astype(jnp.float32).reshape(count_gy, tok_rows, heads_here, head_dim)
        * factor[..., None],
        0,
    )
    attn_part = attn_part.astype(jnp.bfloat16).reshape(tok_rows, heads_here * head_dim)
    (attn,) = exchange([attn_part], "gy", False, 2)
    attn = jnp.swapaxes(attn, 0, 1).reshape(tok_rows, q_cols)
    states_here = lax.dynamic_slice_in_dim(states, col_index * cols_here, cols_here, 1)
    resid = (
        states_here.astype(jnp.float32) + jnp.dot(attn, w_o, preferred_element_type=jnp.float32)
    ).astype(jnp.bfloat16)
    exp_here = w_in.shape[0]
    expert_count = exp_here * count_gx
    top_k = routing.shape[1]
    most_rows = 3 * tok_rows * top_k // (2 * expert_count)
    hidden_units = w_down.shape[1]
    gain_float = ffn_gain.astype(jnp.float32)
    tokens = routing.shape[0]
    slots = count_gx * most_rows
    own_experts = row_index * exp_here + jnp.arange(exp_here, dtype=jnp.int32)
    matched = routing[:, None, :] == own_experts[None, :, None]
    hits = jnp.any(matched, -1)
    weights = jnp.sum(jnp.where(matched, route_weight[:, None, :], 0.0), -1)
    order = jnp.arange(tok_rows, dtype=jnp.int32)
    earlier = (order[:, None] > order[None, :]).astype(jnp.bfloat16)
    rank = jnp.einsum(
        "tu,bue->bte",
        earlier,
        hits.astype(jnp.bfloat16).reshape(count_gx, tok_rows, exp_here),
        preferred_element_type=jnp.float32,
    ).astype(jnp.int32)
    first_slot = jnp.arange(count_gx, dtype=jnp.int32)[:, None, None] * most_rows
    slot_of = jnp.where(hits, (rank + first_slot).reshape(tokens, exp_here), -1)
    pick = slot_of.T[:, None, :] == jnp.arange(slots, dtype=jnp.int32)[None, :, None]
    pick_matrix = pick.astype(jnp.bfloat16)
    slot_weight = jnp.sum(jnp.where(pick, weights.T[:, None, :], 0.0), -1)
    (gathered,) = exchange([resid], "gx", False, 3)
    gathered = gathered.reshape(tokens, cols_here).astype(jnp.float32)
    token_squares = jnp.sum(gathered * gathered, -1)
    slot_squares = jnp.sum(jnp.where(pick, token_squares, 0.0), -1)
    piece = slots // 2
    slot_squares = jnp.pad(slot_squares.reshape(-1, piece), ((0, 0), (0, 128 - piece)))
    scaled = (gathered * gain_float).astype(jnp.bfloat16)
    rows = jnp.einsum(
        "est,td->esd", pick_matrix, scaled, preferred_element_type=jnp.float32
    ).astype(jnp.bfloat16)
    hidden = expert_hidden(rows, slot_squares, w_in, model_width, 4)
    expert_out = jnp.einsum("esf,efd->esd", hidden, w_down, preferred_element_type=jnp.float32)
    expert_out = (expert_out * slot_weight[..., None]).astype(jnp.bfloat16)
    partial_moe = jnp.einsum(
        "est,esd->td", pick_matrix, expert_out, preferred_element_type=jnp.float32
    ).astype(jnp.bfloat16)
    (returned,) = exchange(
        [partial_moe.reshape(count_gx, tok_rows, cols_here)], "gx", True, 5
    )
    moe_total = jnp.sum(returned.astype(jnp.float32), 0)
    layer_out = (resid.astype(jnp.float32) + moe_total).astype(jnp.bfloat16)
    kv_new = jnp.concatenate(
        [
            k_rot.reshape(requests_here, tree_size, kv_cols),
            values_new.reshape(requests_here, tree_size, kv_cols),
        ],
        -1,
    )
    accepted_kv = jnp.einsum(
        "rat,rtc->rac", accept.astype(jnp.bfloat16), kv_new, preferred_element_type=jnp.float32
    ).astype(jnp.bfloat16)
    return (layer_out, accepted_kv)


def solution(mesh):
    in_specs = (
        P("gx", None),
        P(),
        P(None, "gy"),
        P(),
        P(),
        P("gx", "gy", None),
        P("gx", "gy", None),
        P("gx"),
        P("gx", None, None),
        P(None, "gy"),
        P("gy"),
        P(),
        P(),
        P("gx", "gy", None),
        P("gx", None, "gy"),
        P("gx", None, None),
    )
    out_specs = (P("gx", "gy"), P("gx", None, None))
    return jax.shard_map(body, mesh=mesh, in_specs=in_specs, out_specs=out_specs, check_vma=False)
```

time: 286 us -> 402 us (1.41)
  Pallas kernels: 0 us -> 344 us
  waiting for transfers between devices: 81.2 us -> 0 us
  blocking collectives: 52.4 us -> 0 us
  local copies, waits for them, and re-layouts: 39.4 us -> 8.91 us
  other arithmetic: 46 us -> 18.1 us
  starting transfers between devices: 17.2 us -> 0 us
  between operations: 15.7 us -> 1.83 us
    pallas_call x0 -> x6, Pallas kernels: none -> 344 us  [the longest x1 220 us: expert_hidden(): pl.pallas_call(kernel, out_shape=jax.ShapeDtypeStruct((2, chunks, piece,...]
    all_gather x3 -> x0, blocking collectives: 43.1 us -> none  [the longest x2 26.8 us: combined_all(): lax.all_gather(a.astype(kind), axis)]
    unnamed x4 -> x0, waiting for transfers between devices: 37.7 us -> none
    all_gather x2 -> x0, waiting for transfers between devices: 29.7 us -> none  [the longest x1 29.6 us: body(): lax.all_gather(hidden, 'gy', axis=1, tiled=True)]
    all_to_all x2 -> x0, starting transfers between devices: 17.1 us -> none  [the longest x1 12.2 us: body(): lax.all_to_all(outgoing, 'gx', split_axis=0, concat_axis=1, tiled=True)]
    another operation x3 -> x1, other arithmetic: 15.8 us -> 0.1 us  [the longest x1 15.4 us: body(): slot_rank = jnp.cumsum(hit_count, 0) - 1]
    scatter x1 -> x0, local copies, waits for them, and re-layouts: 15.5 us -> none  [body(): slot_table = jnp.full((expert_count * most_rows,), tok_rows, jnp.int32).a...]
    all_to_all x2 -> x0, waiting for transfers between devices: 13.9 us -> none  [the longest x1 11.9 us: body(): lax.all_to_all(outgoing, 'gx', split_axis=0, concat_axis=1, tiled=True)]
  transfers between devices with their start and end apart: 5 -> 0, of which waited for: 4 -> 0; matrix products, arithmetic and copies ran while one was open for 17% -> 0% of each run, Pallas kernels for 0% -> 0%
where the time goes in v1:
time: 402 us; the launch traced here: 400 us
  Pallas kernels  344 us (86%)
  matrix products  27 us (7%)
  other arithmetic  18.1 us (5%)
  local copies, waits for them, and re-layouts  8.91 us (2%)
    pallas_call x1, Pallas kernels, expert_hidden(): pl.pallas_call(kernel, out_shape=jax.ShapeDtypeStruct((2, chunks, piece,...  220 us
    pallas_call x5, Pallas kernels, exchange(): pl.pallas_call(kernel, out_shape=outs, in_specs=[pl.BlockSpec(memory_spac...  124 us

profile of v1, /device:TPU:1, one launch (start us, length us, event | category | flops | bytes accessed | tf_op | source)
XLA Modules:
  0.0 400.1 jit_solution(13077118545246297257)
XLA Ops:
  0.6 0.8 compare_reduce_fusion
  1.8 0.7 convert_element_type.203
  2.5 0.7 convert_element_type.179
  3.2 1.1 fusion.35
  4.3 4.3 %convolution_convert_fusion.refs_0_ = bf16[64,1280]{1,0:T(8,128)(2,1)} fusion(bf16[2048,1280]{1,0:T(8,128)(2,1)} %param.18, bf16[64,2048]{1,0:T(8,128)(2,1)} %param.16, f32[2048]{0:T(1024)S(1)} %convert_element_type.179, f32[64]{0:T(128)S(1)} %add_rsqrt_fusion.2), kind=kOutput, calls=%fused_computation.7 | convolution fusion | flops 336150528 | bytes 5677312 | tf_op jit(solution)/shard_map/dot_general | solution.py:311
  8.6 17.9 %exchange_0.1 = bf16[4,64,1280]{2,1,0:T(8,128)(2,1)} custom-call(bf16[64,1280]{1,0:T(8,128)(2,1)} %convolution_convert_fusion.refs_0_), custom_call_target="tpu_custom_call" | custom-call | tf_op jit(solution)/shard_map/exchange_0/pallas_call | solution.py:59
  26.5 1.1 copy.153
  30.7 0.6 slice_bitcast_fusion.1
  32.0 0.7 fusion.68
  32.7 1.3 reshape.494
  34.1 4.7 %fusion.1 = (f32[64,4,8]{2,0,1:T(8,128)S(1)}, f32[4,64,8,1024]{3,2,1,0:T(8,128)}) fusion(pred[1024]{0:T(1024)(128)(4,1)S(1)} %add_compare_fusion, bf16[64,4,8,128]{3,2,0,1:T(8,128)(2,1)S(1)} %pad_maximum_fusion, bf16[1024,4,128,1]{2,1,0,3:T(4,128)(2,1)S(1)} %bitcast.173), kind=kOutput, calls=%fused_computation.4 | convolution fusion | flops 543160320 | bytes 9970688 | tf_op jit(solution)/shard_map/rtkgd,rskd->rtkgs/dot_general | solution.py:334
  39.6 1.4 fusion.55
  41.2 5.7 %fusion.20 = bf16[1,64,4,8,128]{4,3,1,2,0:T(8,128)(2,1)S(1)} fusion(f32[4,128,64,8]{1,3,2,0:T(8,128)} %fusion.55, bf16[1024,4,128,1]{2,1,0,3:T(4,128)(2,1)S(1)} %bitcast.181, f32[4,64,8,1024]{3,2,1,0:T(8,128)} %get-tuple-element.20, f32[64,4,8]{2,0,1:T(8,128)S(1)} %max.19, pred[1024]{0:T(1024)(128)(4,1)S(1)} %add_compare_fusion), kind=kOutput, calls=%fused_computation.23 | convolution fusion | flops 547880960 | bytes 11019264 | tf_op jit(solution)/shard_map/rtkgs,rskd->rtkgd/dot_general | solution.py:356
  47.0 1.1 reshape.499
  48.0 4.6 %convert_reduce_fusion = f32[64,4,8]{2,0,1:T(8,128)S(1)} fusion(f32[64,4,8]{2,0,1:T(8,128)S(1)} %max.19, f32[4,64,8,1024]{3,2,1,0:T(8,128)} %get-tuple-element.20, pred[1024]{0:T(1024)(128)(4,1)S(1)} %add_compare_fusion), kind=kLoop, calls=%fused_computation.2 | loop fusion | flops 14678016 | bytes 8406016 | tf_op jit(solution)/shard_map/reduce_sum | solution.py:353
  53.1 0.8 reshape.501.refs_1_
  53.9 15.9 %exchange_1.1 = (bf16[4,64,1024]{2,1,0:T(8,128)(2,1)}, f32[4,8,128]{2,1,0:T(8,128)}) custom-call(bf16[4,64,1024]{2,1,0:T(8,128)(2,1)} %bitcast.180, f32[4,8,128]{2,1,0:T(8,128)} %reshape.501.refs_1_), custom_call_target="tpu_custom_call" | custom-call | tf_op jit(solution)/shard_map/exchange_1/pallas_call | solution.py:59
  69.7 0.9 reshape.502
  71.2 1.9 multiply_reduce_fusion.1.refs_0_
  73.1 13.8 %exchange_2.1 = bf16[4,64,1024]{2,1,0:T(8,128)(2,1)} custom-call(bf16[64,1024]{1,0:T(8,128)(2,1)} %multiply_reduce_fusion.1.refs_0_), custom_call_target="tpu_custom_call" | custom-call | tf_op jit(solution)/shard_map/exchange_2/pallas_call | solution.py:59
  86.9 1.1 copy.154
  87.9 3.7 fusion.23.refs_0_
  91.6 14.4 %exchange_3.1 = bf16[8,64,512]{2,1,0:T(8,128)(2,1)} custom-call(bf16[64,512]{1,0:T(8,128)(2,1)} %fusion.23.refs_0_), custom_call_target="tpu_custom_call" | custom-call | tf_op jit(solution)/shard_map/exchange_3/pallas_call | solution.py:59
  106.0 1.1 fusion.27
  107.8 1.2 multiply_reduce_fusion
  109.1 0.6 select_reduce_fusion
  109.8 220.3 %expert_hidden.1 = bf16[2,8,48,768]{3,2,1,0:T(8,128)(2,1)S(1)} custom-call(bf16[8,96,512]{2,1,0:T(8,128)(2,1)S(1)} %fusion.6.x_ref, f32[16,128]{1,0:T(8,128)S(1)} %pad.4.sq_ref, bf16[8,512,1536]{2,1,0:T(8,128)(2,1)} %w_hbm.1), custom_call_target="tpu_custom_call" | custom-call | tf_op jit(solution)/shard_map/expert_hidden/pallas_call | solution.py:232
  330.1 5.2 %fusion.15 = bf16[512,512]{1,0:T(8,128)(2,1)} fusion(bf16[8,96,768]{2,1,0:T(8,128)(2,1)S(1)} %bitcast.170, bf16[8,768,512]{2,1,0:T(8,128)(2,1)} %param.30, f32[8,96]{1,0:T(8,128)S(1)} %get-tuple-element.6, s32[8,512]{1,0:T(8,128)S(1)} %select_bitcast_fusion), kind=kOutput, calls=%fused_computation.20 | convolution fusion | flops 1008074752 | bytes 8014848 | tf_op jit(solution)/shard_map/est,esd->td/dot_general | solution.py:424
  335.3 62.2 %exchange_5.1 = bf16[8,64,512]{2,1,0:T(8,128)(2,1)} custom-call(bf16[8,64,512]{2,1,0:T(8,128)(2,1)} %bitcast.184), custom_call_target="tpu_custom_call" | custom-call | tf_op jit(solution)/shard_map/exchange_5/pallas_call | solution.py:59
  397.5 1.1 convert_reduce_fusion.1
  398.6 0.6 add_convert_fusion.1
  399.4 0.7 fusion.26
  (74 shorter events, 6.3 us)
Async XLA Ops:
  4.3 23.7 %copy-start.7 = (bf16[128]{0:T(256)(128)(2,1)S(1)}, bf16[128]{0:T(256)(128)(2,1)}, u32[]{:S(2)}) copy-start(bf16[128]{0:T(256)(128)(2,1)} %param.19) | copy-start | bytes 772
  8.6 20.4 %copy-start.2 = (s32[1,64,64]{2,1,0:T(8,128)S(1)}, s32[1,64,64]{2,1,0:T(8,128)}, u32[]{:S(2)}) copy-start(s32[1,64,64]{2,1,0:T(8,128)} %param.24) | copy-start | bytes 49156
  27.8 3.7 copy-start.8
  38.7 2.2 copy-start
  73.1 34.6 %copy-start.3 = (s32[512,8]{0,1:T(8,128)S(1)}, s32[512,8]{0,1:T(8,128)}, u32[]{:S(2)}) copy-start(s32[512,8]{0,1:T(8,128)} %param.27) | copy-start | bytes 49156
  73.1 34.6 %copy-start.5 = (f32[512,8]{0,1:T(8,128)S(1)}, f32[512,8]{0,1:T(8,128)}, u32[]{:S(2)}) copy-start(f32[512,8]{0,1:T(8,128)} %param.28) | copy-start | bytes 49156
  330.1 68.5 %copy-start.1 = (bf16[64,512]{1,0:T(8,128)(2,1)S(1)}, bf16[64,512]{1,0:T(8,128)(2,1)}, u32[]{:S(2)}) copy-start(bf16[64,512]{1,0:T(8,128)(2,1)} %fusion.23.refs_0_) | copy-start | bytes 196612
  330.1 69.3 %copy-start.4 = (bf16[1,64,512]{2,1,0:T(8,128)(2,1)S(1)}, bf16[1,64,512]{2,1,0:T(8,128)(2,1)}, u32[]{:S(2)}) copy-start(bf16[1,64,512]{2,1,0:T(8,128)(2,1)} %get-tuple-element.12) | copy-start | bytes 196612
  330.1 69.3 %copy-start.6 = (s32[1,8,64]{2,1,0:T(8,128)S(1)}, s32[1,8,64]{2,1,0:T(8,128)}, u32[]{:S(2)}) copy-start(s32[1,8,64]{2,1,0:T(8,128)} %param.31) | copy-start | bytes 6148

commit v2 on v1

--- a/solution.py
+++ b/solution.py
@@ -78,10 +78,11 @@
     wide = w_in.shape[2]
     units = wide // 2
     half = experts // 2
-    sub = 2
-    piece = slots // sub
+    piece = 16
+    sub = slots // piece
     chunks = half * sub
-    lag = 2
+    hop = 2
+    far = hop * (count - 1)
 
     def kernel(
         x_ref, sq_ref, w_hbm, hid_ref, wbuf, part, rbuf, sqbuf, inv_ref,
@@ -188,30 +189,38 @@
             def _():
                 hid_copy(h, c).start()
 
-        def step(s, carry):
-            @pl.when(s < half)
-            def _():
-                for h in (1, 0):
-                    e = h * half + s
-                    load(e).wait()
-                    value = jnp.dot(x_ref[e], wbuf[e], preferred_element_type=jnp.float32)
-                    for j in range(sub):
-                        part[h, s * sub + j] = value[j * piece : (j + 1) * piece].astype(
-                            jnp.bfloat16
-                        )
+        def multiply(s):
+            for h in (1, 0):
+                e = h * half + s
+                load(e).wait()
+                value = jnp.dot(x_ref[e], wbuf[e], preferred_element_type=jnp.float32)
                 for j in range(sub):
-                    for h in (1, 0):
-                        reduce_chunk(h, s * sub + j)
-
-            @pl.when(s >= lag)
-            def _():
-                for j in range(sub):
-                    for h in (1, 0):
-                        return_chunk(h, (s - lag) * sub + j)
+                    part[h, s * sub + j] = value[j * piece : (j + 1) * piece].astype(jnp.bfloat16)
+
+        def step(t, carry):
+            @pl.when(jnp.logical_and(t < chunks, lax.rem(t, sub) == 0))
+            def _():
+                multiply(lax.div(t, sub))
+
+            for h in (1, 0):
+                way = hop * (me if h else count - 1 - me)
+                c = t - way
+
+                @pl.when(jnp.logical_and(c >= 0, c < chunks))
+                def _():
+                    reduce_chunk(h, c)
+
+            for h in (1, 0):
+                way = hop * (me if h else count - 1 - me)
+                b = t - 2 * far + way
+
+                @pl.when(jnp.logical_and(b >= 0, b < chunks))
+                def _():
+                    return_chunk(h, b)
 
             return carry
 
-        lax.fori_loop(0, half + lag, step, 0)
+        lax.fori_loop(0, chunks + 2 * far, step, 0)
 
         def finish(c, carry):
             for h in (1, 0):
@@ -260,19 +269,113 @@
     return hidden.reshape(experts, slots, units)
 
 
+def attend(qkv, q_gain, k_gain, cosine, sine, cache_k, cache_v, bounds, tree_mask, blocks):
+    tokens = qkv.shape[0]
+    span, kv_cols = cache_k.shape
+    dim = q_gain.shape[1]
+    kv_heads = kv_cols // dim
+    heads = qkv.shape[1] // dim - 2 * kv_heads
+    group = heads // kv_heads
+    per_block = heads // blocks
+    blocks_here = blocks // kv_heads
+    scale = dim ** (-0.5)
+
+    def kernel(
+        bounds_ref, q_ref, kn_ref, vn_ref, qg_ref, kg_ref, cos_ref, sin_ref, k_ref, v_ref,
+        mask_ref, acc_ref, stat_ref, rot_ref,
+    ):
+        cos = cos_ref[...]
+        sin = sin_ref[...]
+
+        def turn(value, gain):
+            value = value.astype(jnp.float32)
+            value = value * lax.rsqrt(jnp.mean(value * value, -1, keepdims=True) + EPS) * gain
+            return (value * cos + pltpu.roll(value, dim // 2, 1) * sin).astype(jnp.bfloat16)
+
+        gain = qg_ref[...].astype(jnp.float32)
+        query = jnp.concatenate(
+            [turn(q_ref[:, i * dim : (i + 1) * dim], gain) for i in range(group)], 0
+        )
+        keys = turn(kn_ref[...], kg_ref[...].astype(jnp.float32))
+        rot_ref[...] = keys
+        contract = (((1,), (1,)), ((), ()))
+        tree = (
+            lax.dot_general(query, keys, contract, preferred_element_type=jnp.float32) * scale
+        )
+        mask = jnp.concatenate([mask_ref[...]] * group, 0)
+        tree_ok = jnp.logical_and(mask == 1, bounds_ref[1] == 0)
+        tree = jnp.where(tree_ok, tree, NEG)
+        score = (
+            lax.dot_general(query, k_ref[...], contract, preferred_element_type=jnp.float32)
+            * scale
+        )
+        valid = lax.broadcasted_iota(jnp.int32, score.shape, 1) < bounds_ref[0]
+        score = jnp.where(valid, score, NEG)
+        top = jnp.maximum(
+            jnp.max(score, 1, keepdims=True), jnp.max(tree, 1, keepdims=True)
+        )
+        prob = jnp.where(valid, jnp.exp(score - top), 0.0).astype(jnp.bfloat16)
+        prob_tree = jnp.where(tree_ok, jnp.exp(tree - top), 0.0).astype(jnp.bfloat16)
+        total = jnp.sum(prob.astype(jnp.float32), 1, keepdims=True) + jnp.sum(
+            prob_tree.astype(jnp.float32), 1, keepdims=True
+        )
+        acc = jnp.dot(prob, v_ref[...], preferred_element_type=jnp.float32)
+        acc = acc + jnp.dot(prob_tree, vn_ref[...], preferred_element_type=jnp.float32)
+        acc = acc.astype(jnp.bfloat16)
+        diagonal = lax.broadcasted_iota(jnp.int32, (tokens, 128), 0) == lax.broadcasted_iota(
+            jnp.int32, (tokens, 128), 1
+        )
+        for i in range(group):
+            rows = slice(i * tokens, (i + 1) * tokens)
+            block, place = divmod(i, per_block)
+            acc_ref[block, :, place * dim : (place + 1) * dim] = acc[rows]
+            for j, column in enumerate((top, total)):
+                stat_ref[block, j * per_block + place : j * per_block + place + 1, :] = jnp.sum(
+                    jnp.where(diagonal, column[rows], 0.0), 0, keepdims=True
+                )
+
+    whole = lambda shape: pl.BlockSpec(shape, lambda g: (0,) * len(shape))
+    return pl.pallas_call(
+        kernel,
+        grid=(kv_heads,),
+        out_shape=[
+            jax.ShapeDtypeStruct((blocks, tokens, per_block * dim), jnp.bfloat16),
+            jax.ShapeDtypeStruct((blocks, 2 * per_block, 128), jnp.float32),
+            jax.ShapeDtypeStruct((tokens, kv_cols), jnp.bfloat16),
+        ],
+        in_specs=[
+            pl.BlockSpec(memory_space=pltpu.SMEM),
+            pl.BlockSpec((tokens, group * dim), lambda g: (0, g)),
+            pl.BlockSpec((tokens, dim), lambda g: (0, heads + g)),
+            pl.BlockSpec((tokens, dim), lambda g: (0, heads + kv_heads + g)),
+            whole((1, dim)),
+            whole((1, dim)),
+            whole((tokens, dim)),
+            whole((tokens, dim)),
+            pl.BlockSpec((span, dim), lambda g: (0, g)),
+            pl.BlockSpec((span, dim), lambda g: (0, g)),
+            whole((tokens, tokens)),
+        ],
+        out_specs=[
+            pl.BlockSpec((blocks_here, tokens, per_block * dim), lambda g: (g, 0, 0)),
+            pl.BlockSpec((blocks_here, 2 * per_block, 128), lambda g: (g, 0, 0)),
+            pl.BlockSpec((tokens, dim), lambda g: (0, g)),
+        ],
+        compiler_params=pltpu.CompilerParams(vmem_limit_bytes=40 * 1024 * 1024),
+        name="attend",
+    )(bounds, qkv, qkv, qkv, q_gain, k_gain, cosine, sine, cache_k, cache_v, tree_mask)
+
+
 def rms_scale(values, gain):
     return values * lax.rsqrt(jnp.mean(values * values, -1, keepdims=True) + EPS) * gain
 
 
-def rotate(values, position):
-    half = values.shape[-1] // 2
-    freqs = jnp.exp(jnp.arange(half, dtype=jnp.float32) * (-2.0 * THETA_LOG / values.shape[-1]))
+def angles_of(position, dim):
+    freqs = jnp.exp(jnp.arange(dim // 2, dtype=jnp.float32) * (-2.0 * THETA_LOG / dim))
     angles = position.astype(jnp.float32)[..., None] * freqs
     cosine = jnp.cos(angles)
     sine = jnp.sin(angles)
-    lower = values[..., :half]
-    upper = values[..., half:]
-    return jnp.concatenate([lower * cosine - upper * sine, upper * cosine + lower * sine], -1)
+    return jnp.concatenate([cosine, cosine], -1), jnp.concatenate([-sine, sine], -1)
 
 
 def body(
@@ -296,10 +399,7 @@
     tok_rows, model_width = states.shape
     head_dim = q_gain.shape[0]
     kv_cols = cache_k.shape[2]
-    kv_heads = kv_cols // head_dim
     heads_all = w_o.shape[0] // head_dim
-    group = heads_all // kv_heads
-    requests_here, tree_size = (tree_mask.shape[0], tree_mask.shape[1])
     cache_span = cache_k.shape[1]
     cols_here = w_o.shape[1]
     col_index = lax.axis_index("gy")
@@ -312,62 +412,26 @@
     (qkv_blocks,) = exchange([qkv_part], "gy", False, 0)
     qkv_whole = jnp.swapaxes(qkv_blocks, 0, 1).reshape(tok_rows, -1)
     q_cols = heads_all * head_dim
-    query = qkv_whole[:, :q_cols].reshape(requests_here, tree_size, kv_heads, group, head_dim)
-    keys_new = qkv_whole[:, q_cols : q_cols + kv_cols].reshape(
-        requests_here, tree_size, kv_heads, head_dim
-    )
-    values_new = qkv_whole[:, q_cols + kv_cols :].reshape(
-        requests_here, tree_size, kv_heads, head_dim
-    )
     depth = jnp.sum(tree_mask, -1) - 1
-    position = cache_len[:, None] + depth
-    q_rot = rotate(
-        rms_scale(query.astype(jnp.float32), q_gain.astype(jnp.float32)), position[:, :, None, None]
-    ).astype(jnp.bfloat16)
-    k_rot = rotate(
-        rms_scale(keys_new.astype(jnp.float32), k_gain.astype(jnp.float32)), position[:, :, None]
-    ).astype(jnp.bfloat16)
-    cached_keys = cache_k.reshape(requests_here, cache_span, kv_heads, head_dim)
-    cached_values = cache_v.reshape(requests_here, cache_span, kv_heads, head_dim)
-    score_scale = head_dim ** (-0.5)
-    scores_cache = (
-        jnp.einsum("rtkgd,rskd->rtkgs", q_rot, cached_keys, preferred_element_type=jnp.float32)
-        * score_scale
-    )
-    scores_tree = (
-        jnp.einsum("rtkgd,rukd->rtkgu", q_rot, k_rot, preferred_element_type=jnp.float32)
-        * score_scale
-    )
-    cache_pos = col_index * cache_span + jnp.arange(cache_span, dtype=jnp.int32)
-    valid = (cache_pos[None, :] < cache_len[:, None])[:, None, None, None, :]
-    tree_ok = ((tree_mask == 1) & (col_index == 0))[:, :, None, None, :]
-    scores_cache = jnp.where(valid, scores_cache, NEG)
-    scores_tree = jnp.where(tree_ok, scores_tree, NEG)
-    row_max = jnp.maximum(jnp.max(scores_cache, -1), jnp.max(scores_tree, -1))
-    probs_cache = jnp.where(valid, jnp.exp(scores_cache - row_max[..., None]), 0.0).astype(
-        jnp.bfloat16
-    )
-    probs_tree = jnp.where(tree_ok, jnp.exp(scores_tree - row_max[..., None]), 0.0).astype(
-        jnp.bfloat16
-    )
-    denom_sum = jnp.sum(probs_cache.astype(jnp.float32), -1) + jnp.sum(
-        probs_tree.astype(jnp.float32), -1
-    )
-    weighted = jnp.einsum(
-        "rtkgs,rskd->rtkgd", probs_cache, cached_values, preferred_element_type=jnp.float32
-    )
-    weighted = weighted + jnp.einsum(
-        "rtkgu,rukd->rtkgd", probs_tree, values_new, preferred_element_type=jnp.float32
-    )
+    cosine, sine = angles_of((cache_len[:, None] + depth)[0], head_dim)
+    bounds = jnp.concatenate([cache_len - col_index * cache_span, col_index[None]])
     count_gy = lax.axis_size("gy")
     heads_here = heads_all // count_gy
-    blocks = jnp.swapaxes(
-        weighted.astype(jnp.bfloat16).reshape(tok_rows, count_gy, heads_here * head_dim), 0, 1
+    blocks, stats, k_rot = attend(
+        qkv_whole,
+        q_gain[None],
+        k_gain[None],
+        cosine,
+        sine,
+        cache_k[0],
+        cache_v[0],
+        bounds,
+        tree_mask[0],
+        count_gy,
     )
-    stats = jnp.stack([row_max, denom_sum]).reshape(2, tok_rows, count_gy, heads_here)
-    stats = stats.transpose(2, 0, 1, 3).reshape(count_gy, -1, 128)
     blocks, stats = exchange([blocks, stats], "gy", True, 1)
-    stats = stats.reshape(count_gy, 2, tok_rows, heads_here)
+    stats = stats[:, :, :tok_rows].reshape(count_gy, 2, heads_here, tok_rows)
+    stats = jnp.swapaxes(stats, 2, 3)
     factor = jnp.exp(stats[:, 0] - jnp.max(stats[:, 0], 0))
     denom = jnp.sum(stats[:, 1] * factor, 0)
     factor = factor / denom
@@ -412,7 +476,7 @@
     gathered = gathered.reshape(tokens, cols_here).astype(jnp.float32)
     token_squares = jnp.sum(gathered * gathered, -1)
     slot_squares = jnp.sum(jnp.where(pick, token_squares, 0.0), -1)
-    piece = slots // 2
+    piece = 16
     slot_squares = jnp.pad(slot_squares.reshape(-1, piece), ((0, 0), (0, 128 - piece)))
     scaled = (gathered * gain_float).astype(jnp.bfloat16)
     rows = jnp.einsum(
@@ -429,13 +493,7 @@
     )
     moe_total = jnp.sum(returned.astype(jnp.float32), 0)
     layer_out = (resid.astype(jnp.float32) + moe_total).astype(jnp.bfloat16)
-    kv_new = jnp.concatenate(
-        [
-            k_rot.reshape(requests_here, tree_size, kv_cols),
-            values_new.reshape(requests_here, tree_size, kv_cols),
-        ],
-        -1,
-    )
+    kv_new = jnp.concatenate([k_rot, qkv_whole[:, q_cols + kv_cols :]], -1)[None]
     accepted_kv = jnp.einsum(
         "rat,rtc->rac", accept.astype(jnp.bfloat16), kv_new, preferred_element_type=jnp.float32
     ).astype(jnp.bfloat16)

time: 402 us -> 184 us (0.46)
  Pallas kernels: 344 us -> 150 us
  matrix products: 27 us -> 14.5 us
  other arithmetic: 18.1 us -> 11 us
    pallas_call x1, Pallas kernels: 220 us -> 57.6 us  [expert_hidden(): pl.pallas_call(kernel, out_shape=jax.ShapeDtypeStruct((2, chunks, piece,...]
    pallas_call x5, Pallas kernels: 124 us -> 82.8 us  [exchange(): pl.pallas_call(kernel, out_shape=outs, in_specs=[pl.BlockSpec(memory_spac...]
    dot_general x4 -> x0, matrix products: 12.4 us -> none  [the longest x1 5.72 us: body(): jnp.einsum('rtkgs,rskd->rtkgd', probs_cache, cached_values, preferred_ele...]
    pallas_call x0 -> x1, Pallas kernels: none -> 9.55 us  [attend(): pl.pallas_call(kernel, grid=(kv_heads,), out_shape=[jax.ShapeDtypeStruct(...]
    reduce_sum x2 -> x0, other arithmetic: 4.93 us -> none  [the longest x1 4.63 us: body(): jnp.sum(probs_cache.astype(jnp.float32), -1)]
where the time goes in v2:
time: 184 us; the launch traced here: 183 us
  Pallas kernels  150 us (82%)
  matrix products  14.5 us (8%)
  other arithmetic  11 us (6%)
  local copies, waits for them, and re-layouts  5.89 us (3%)
    pallas_call x5, Pallas kernels, exchange(): pl.pallas_call(kernel, out_shape=outs, in_specs=[pl.BlockSpec(memory_spac...  82.8 us
    pallas_call x1, Pallas kernels, expert_hidden(): pl.pallas_call(kernel, out_shape=jax.ShapeDtypeStruct((2, chunks, piece,...  57.6 us
    pallas_call x1, Pallas kernels, attend(): pl.pallas_call(kernel, grid=(kv_heads,), out_shape=[jax.ShapeDtypeStruct(...  9.55 us
    dot_general x1, matrix products, body(): jnp.einsum('est,esd->td', pick_matrix, expert_out, preferred_element_type...  5.13 us
    dot_general x1, matrix products, body(): jnp.dot(normed, w_qkv, preferred_element_type=jnp.float32)  4.32 us

profile of v2, /device:TPU:1, one launch (start us, length us, event | category | flops | bytes accessed | tf_op | source)
XLA Modules:
  0.0 182.9 jit_solution(12389728386903575802)
XLA Ops:
  1.4 0.9 reduce_sum.84
  2.2 1.1 fusion.13
  3.4 0.7 convert_element_type.99
  4.1 0.8 compare_reduce_fusion
  5.0 0.7 convert_element_type.88
  5.7 0.8 fusion.20
  6.8 0.2 fusion.31
  7.1 4.3 %convolution_convert_fusion.refs_0_ = bf16[64,1280]{1,0:T(8,128)(2,1)} fusion(bf16[2048,1280]{1,0:T(8,128)(2,1)} %param.18, bf16[64,2048]{1,0:T(8,128)(2,1)} %param.16, f32[2048]{0:T(1024)S(1)} %convert_element_type.88, f32[64]{0:T(128)S(1)} %add_rsqrt_fusion), kind=kOutput, calls=%fused_computation | convolution fusion | flops 336150528 | bytes 5677312 | tf_op jit(solution)/shard_map/dot_general | solution.py:411
  11.4 18.0 %exchange_0.1 = bf16[4,64,1280]{2,1,0:T(8,128)(2,1)} custom-call(bf16[64,1280]{1,0:T(8,128)(2,1)} %convolution_convert_fusion.refs_0_), custom_call_target="tpu_custom_call" | custom-call | tf_op jit(solution)/shard_map/exchange_0/pallas_call | solution.py:59
  29.5 1.1 copy.38
  30.7 9.5 %attend.1 = (bf16[4,64,1024]{2,1,0:T(8,128)(2,1)S(1)}, f32[4,16,128]{2,1,0:T(8,128)S(1)}, bf16[64,512]{1,0:T(8,128)(2,1)S(1)}) custom-call(s32[2]{0:T(128)S(1)} %pad_add_fusion.bounds_ref, bf16[64,5120]{1,0:T(8,128)(2,1)S(1)} %bitcast.76, bf16[64,5120]{1,0:T(8,128)(2,1)S(1)} %bitcast.77, bf16[64,5120]{1,0:T(8,128)(2,1)S(1)} %bitcast.78, ...), custom_call_target="tpu_custom_call" | custom-call | tf_op jit(solution)/shard_map/attend/pallas_call | solution.py:338
  40.2 0.8 copy-done.2
  41.0 0.6 copy-done.4
  41.6 0.7 fusion.8
  42.4 16.2 %exchange_1.1 = (bf16[4,64,1024]{2,1,0:T(8,128)(2,1)}, f32[4,16,128]{2,1,0:T(8,128)}) custom-call(bf16[4,64,1024]{2,1,0:T(8,128)(2,1)} %copy-done.2, f32[4,16,128]{2,1,0:T(8,128)} %copy-done.4), custom_call_target="tpu_custom_call" | custom-call | tf_op jit(solution)/shard_map/exchange_1/pallas_call | solution.py:59
  58.5 0.8 slice_bitcast_fusion
  59.5 0.3 mul.106
  60.0 0.5 copy-done.8
  60.5 0.8 multiply_reduce_fusion.1.refs_0_
  61.3 14.0 %exchange_2.1 = bf16[4,64,1024]{2,1,0:T(8,128)(2,1)} custom-call(bf16[64,1024]{1,0:T(8,128)(2,1)} %multiply_reduce_fusion.1.refs_0_), custom_call_target="tpu_custom_call" | custom-call | tf_op jit(solution)/shard_map/exchange_2/pallas_call | solution.py:59
  75.3 1.1 copy.39
  76.4 3.7 %fusion.5.refs_0_ = bf16[64,512]{1,0:T(8,128)(2,1)} fusion(bf16[64,4096]{1,0:T(8,128)(2,1)S(1)} %bitcast.86, bf16[4096,512]{1,0:T(8,128)(2,1)} %param.25, bf16[64,2048]{1,0:T(8,128)(2,1)} %param.16, s32[]{:T(128)S(6)} %select_n.19), kind=kOutput, calls=%fused_computation.11 | convolution fusion | flops 268533760 | bytes 4849668 | tf_op jit(solution)/shard_map/dot_general | solution.py:448
  80.1 14.1 %exchange_3.1 = bf16[8,64,512]{2,1,0:T(8,128)(2,1)} custom-call(bf16[64,512]{1,0:T(8,128)(2,1)} %fusion.5.refs_0_), custom_call_target="tpu_custom_call" | custom-call | tf_op jit(solution)/shard_map/exchange_3/pallas_call | solution.py:59
  94.2 1.2 multiply_reduce_fusion
  95.4 1.1 fusion.9
  96.6 0.6 select_reduce_fusion
  97.3 0.6 fusion.2.x_ref
  97.9 57.6 %expert_hidden.1 = bf16[2,24,16,768]{3,2,1,0:T(8,128)(2,1)S(1)} custom-call(bf16[8,96,512]{2,1,0:T(8,128)(2,1)S(1)} %fusion.2.x_ref, f32[48,128]{1,0:T(8,128)S(1)} %pad.4.sq_ref, bf16[8,512,1536]{2,1,0:T(8,128)(2,1)} %w_hbm.1), custom_call_target="tpu_custom_call" | custom-call | tf_op jit(solution)/shard_map/expert_hidden/pallas_call | solution.py:241
  155.5 5.1 %fusion.4 = bf16[512,512]{1,0:T(8,128)(2,1)} fusion(bf16[8,96,768]{2,1,0:T(8,128)(2,1)S(1)} %bitcast.79, bf16[8,768,512]{2,1,0:T(8,128)(2,1)} %param.30, f32[8,96]{1,0:T(8,128)S(1)} %get-tuple-element.12, s32[8,512]{1,0:T(8,128)S(1)} %select_bitcast_fusion), kind=kOutput, calls=%fused_computation.9 | convolution fusion | flops 1008074752 | bytes 8014848 | tf_op jit(solution)/shard_map/est,esd->td/dot_general | solution.py:488
  160.6 20.5 %exchange_5.1 = bf16[8,64,512]{2,1,0:T(8,128)(2,1)} custom-call(bf16[8,64,512]{2,1,0:T(8,128)(2,1)} %bitcast.88), custom_call_target="tpu_custom_call" | custom-call | tf_op jit(solution)/shard_map/exchange_5/pallas_call | solution.py:59
  181.2 1.1 convert_reduce_fusion
  182.3 0.6 add_convert_fusion
  (38 shorter events, 1.0 us)
Async XLA Ops:
  11.4 19.2 %copy-start = (bf16[1,1024,512]{2,1,0:T(8,128)(2,1)S(1)}, bf16[1,1024,512]{2,1,0:T(8,128)(2,1)}, u32[]{:S(2)}) copy-start(bf16[1,1024,512]{2,1,0:T(8,128)(2,1)} %param.21) | copy-start | bytes 3145732
  11.4 19.2 %copy-start.1 = (bf16[1,1024,512]{2,1,0:T(8,128)(2,1)S(1)}, bf16[1,1024,512]{2,1,0:T(8,128)(2,1)}, u32[]{:S(2)}) copy-start(bf16[1,1024,512]{2,1,0:T(8,128)(2,1)} %param.22) | copy-start | bytes 3145732
  11.4 19.2 %copy-start.3 = (s32[1,64,64]{2,1,0:T(8,128)S(1)}, s32[1,64,64]{2,1,0:T(8,128)}, u32[]{:S(2)}) copy-start(s32[1,64,64]{2,1,0:T(8,128)} %param.24) | copy-start | bytes 49156
  11.4 19.2 %copy-start.5 = (bf16[128]{0:T(256)(128)(2,1)S(1)}, bf16[128]{0:T(256)(128)(2,1)}, u32[]{:S(2)}) copy-start(bf16[128]{0:T(256)(128)(2,1)} %param.19) | copy-start | bytes 772
  11.4 19.2 %copy-start.6 = (bf16[128]{0:T(256)(128)(2,1)S(1)}, bf16[128]{0:T(256)(128)(2,1)}, u32[]{:S(2)}) copy-start(bf16[128]{0:T(256)(128)(2,1)} %param.20) | copy-start | bytes 772
  30.7 11.0 %copy-start.9 = (s32[1,8,64]{2,1,0:T(8,128)S(1)}, s32[1,8,64]{2,1,0:T(8,128)}, u32[]{:S(2)}) copy-start(s32[1,8,64]{2,1,0:T(8,128)} %param.31) | copy-start | bytes 6148
  40.2 0.8 copy-start.2
  41.0 0.6 copy-start.4
  59.5 1.0 copy-start.8
  160.6 21.6 %copy-start.7 = (bf16[64,512]{1,0:T(8,128)(2,1)S(1)}, bf16[64,512]{1,0:T(8,128)(2,1)}, u32[]{:S(2)}) copy-start(bf16[64,512]{1,0:T(8,128)(2,1)} %fusion.5.refs_0_) | copy-start | bytes 196612

commit v3 on v2

--- a/solution.py
+++ b/solution.py
@@ -269,7 +269,11 @@
     return hidden.reshape(experts, slots, units)
 
 
-def attend(qkv, q_gain, k_gain, cosine, sine, cache_k, cache_v, bounds, tree_mask, blocks):
+def attention_block(
+    qkv, q_gain, k_gain, cosine, sine, cache_k, cache_v, limit, tree_mask, states_here, w_o, cid
+):
+    blocks = lax.axis_size("gy")
+    rows_gx = lax.axis_size("gx")
     tokens = qkv.shape[0]
     span, kv_cols = cache_k.shape
     dim = q_gain.shape[1]
@@ -278,12 +282,44 @@
     group = heads // kv_heads
     per_block = heads // blocks
     blocks_here = blocks // kv_heads
+    width = per_block * dim
+    cols = w_o.shape[1]
     scale = dim ** (-0.5)
 
     def kernel(
-        bounds_ref, q_ref, kn_ref, vn_ref, qg_ref, kg_ref, cos_ref, sin_ref, k_ref, v_ref,
-        mask_ref, acc_ref, stat_ref, rot_ref,
+        limit_ref, q_ref, qg_ref, kg_ref, cos_ref, sin_ref, k_ref, v_ref, mask_ref, st_ref, wo_hbm,
+        h_ref, rot_ref,
+        acc_out, stat_out, acc_in, stat_in, attn, wo,
+        wo_sem, a_s, a_r, s_s, s_r, t_s, t_r, h_s, h_r,
     ):
+        me = lax.axis_index("gy")
+        row = lax.axis_index("gx")
+        load = pltpu.make_async_copy(wo_hbm, wo, wo_sem)
+        load.start()
+        barrier = pltpu.get_barrier_semaphore()
+        for axis, here, count in (("gy", me, blocks), ("gx", row, rows_gx)):
+            for d in range(1, count):
+                pl.semaphore_signal(
+                    barrier, inc=1, device_id={axis: lax.rem(here + d, count)}, device_id_type=MESH
+                )
+        pl.semaphore_wait(barrier, blocks + rows_gx - 2)
+
+        def send(src, dst, send_sem, recv_sem, axis, peer):
+            return pltpu.make_async_remote_copy(
+                src_ref=src,
+                dst_ref=dst,
+                send_sem=send_sem,
+                recv_sem=recv_sem,
+                device_id={axis: peer},
+                device_id_type=MESH,
+            )
+
+        def part_copies(block, source):
+            return (
+                send(acc_out.at[block], acc_in.at[source], a_s.at[block], a_r.at[source], "gy", block),
+                send(stat_out.at[block], stat_in.at[source], s_s.at[block], s_r.at[source], "gy", block),
+            )
+
         cos = cos_ref[...]
         sin = sin_ref[...]
 
@@ -292,78 +328,175 @@
             value = value * lax.rsqrt(jnp.mean(value * value, -1, keepdims=True) + EPS) * gain
             return (value * cos + pltpu.roll(value, dim // 2, 1) * sin).astype(jnp.bfloat16)
 
-        gain = qg_ref[...].astype(jnp.float32)
-        query = jnp.concatenate(
-            [turn(q_ref[:, i * dim : (i + 1) * dim], gain) for i in range(group)], 0
-        )
-        keys = turn(kn_ref[...], kg_ref[...].astype(jnp.float32))
-        rot_ref[...] = keys
+        q_gain_row = qg_ref[...].astype(jnp.float32)
+        k_gain_row = kg_ref[...].astype(jnp.float32)
         contract = (((1,), (1,)), ((), ()))
-        tree = (
-            lax.dot_general(query, keys, contract, preferred_element_type=jnp.float32) * scale
-        )
-        mask = jnp.concatenate([mask_ref[...]] * group, 0)
-        tree_ok = jnp.logical_and(mask == 1, bounds_ref[1] == 0)
-        tree = jnp.where(tree_ok, tree, NEG)
-        score = (
-            lax.dot_general(query, k_ref[...], contract, preferred_element_type=jnp.float32)
-            * scale
-        )
-        valid = lax.broadcasted_iota(jnp.int32, score.shape, 1) < bounds_ref[0]
-        score = jnp.where(valid, score, NEG)
-        top = jnp.maximum(
-            jnp.max(score, 1, keepdims=True), jnp.max(tree, 1, keepdims=True)
-        )
-        prob = jnp.where(valid, jnp.exp(score - top), 0.0).astype(jnp.bfloat16)
-        prob_tree = jnp.where(tree_ok, jnp.exp(tree - top), 0.0).astype(jnp.bfloat16)
-        total = jnp.sum(prob.astype(jnp.float32), 1, keepdims=True) + jnp.sum(
-            prob_tree.astype(jnp.float32), 1, keepdims=True
-        )
-        acc = jnp.dot(prob, v_ref[...], preferred_element_type=jnp.float32)
-        acc = acc + jnp.dot(prob_tree, vn_ref[...], preferred_element_type=jnp.float32)
-        acc = acc.astype(jnp.bfloat16)
         diagonal = lax.broadcasted_iota(jnp.int32, (tokens, 128), 0) == lax.broadcasted_iota(
             jnp.int32, (tokens, 128), 1
         )
-        for i in range(group):
-            rows = slice(i * tokens, (i + 1) * tokens)
-            block, place = divmod(i, per_block)
-            acc_ref[block, :, place * dim : (place + 1) * dim] = acc[rows]
-            for j, column in enumerate((top, total)):
-                stat_ref[block, j * per_block + place : j * per_block + place + 1, :] = jnp.sum(
-                    jnp.where(diagonal, column[rows], 0.0), 0, keepdims=True
+
+        def one_head(i, carry):
+            g = lax.rem(lax.div(me, blocks_here) + 1 + i, kv_heads)
+
+            def lanes(first, size):
+                return pl.ds(pl.multiple_of(first, 128), size)
+
+            query = jnp.concatenate(
+                [
+                    turn(q_ref[:, lanes((g * group + j) * dim, dim)], q_gain_row)
+                    for j in range(group)
+                ],
+                0,
+            )
+            keys = turn(q_ref[:, lanes((heads + g) * dim, dim)], k_gain_row)
+            values = q_ref[:, lanes((heads + kv_heads + g) * dim, dim)]
+            rot_ref[:, lanes(g * dim, dim)] = keys
+            tree = (
+                lax.dot_general(query, keys, contract, preferred_element_type=jnp.float32) * scale
+            )
+            mask = jnp.concatenate([mask_ref[...]] * group, 0)
+            tree_ok = jnp.logical_and(mask == 1, me == 0)
+            tree = jnp.where(tree_ok, tree, NEG)
+            score = (
+                lax.dot_general(
+                    query,
+                    k_ref[:, lanes(g * dim, dim)],
+                    contract,
+                    preferred_element_type=jnp.float32,
                 )
-
-    whole = lambda shape: pl.BlockSpec(shape, lambda g: (0,) * len(shape))
+                * scale
+            )
+            valid = lax.broadcasted_iota(jnp.int32, score.shape, 1) < limit_ref[0]
+            score = jnp.where(valid, score, NEG)
+            top = jnp.maximum(jnp.max(score, 1, keepdims=True), jnp.max(tree, 1, keepdims=True))
+            prob = jnp.where(valid, jnp.exp(score - top), 0.0).astype(jnp.bfloat16)
+            prob_tree = jnp.where(tree_ok, jnp.exp(tree - top), 0.0).astype(jnp.bfloat16)
+            total = jnp.sum(prob.astype(jnp.float32), 1, keepdims=True) + jnp.sum(
+                prob_tree.astype(jnp.float32), 1, keepdims=True
+            )
+            acc = jnp.dot(prob, v_ref[:, lanes(g * dim, dim)], preferred_element_type=jnp.float32)
+            acc = acc + jnp.dot(prob_tree, values, preferred_element_type=jnp.float32)
+            acc = acc.astype(jnp.bfloat16)
+            for b in range(blocks_here):
+                block = g * blocks_here + b
+                for place in range(per_block):
+                    j = b * per_block + place
+                    rows = slice(j * tokens, (j + 1) * tokens)
+                    acc_out[block, :, place * dim : (place + 1) * dim] = acc[rows]
+                    for k, column in enumerate((top, total)):
+                        stat_out[block, k * per_block + place : k * per_block + place + 1, :] = (
+                            jnp.sum(jnp.where(diagonal, column[rows], 0.0), 0, keepdims=True)
+                        )
+
+                @pl.when(block != me)
+                def _():
+                    for copy in part_copies(block, me):
+                        copy.start()
+
+            return carry
+
+        lax.fori_loop(0, kv_heads, one_head, 0)
+
+        acc_in[me] = acc_out[me]
+        stat_in[me] = stat_out[me]
+        for d in range(1, blocks):
+            source = lax.rem(me + d, blocks)
+            for copy in part_copies(source, source):
+                copy.wait_recv()
+        tops = [stat_in[j, :per_block, :] for j in range(blocks)]
+        best = tops[0]
+        for j in range(1, blocks):
+            best = jnp.maximum(best, tops[j])
+        factors = [jnp.exp(tops[j] - best) for j in range(blocks)]
+        denom = stat_in[0, per_block:, :] * factors[0]
+        for j in range(1, blocks):
+            denom = denom + stat_in[j, per_block:, :] * factors[j]
+        for place in range(per_block):
+            joined = jnp.zeros((tokens, dim), jnp.float32)
+            for j in range(blocks):
+                line = (factors[j] / denom)[place : place + 1, :]
+                column = jnp.sum(jnp.where(diagonal, line, 0.0), 1, keepdims=True)
+                joined = joined + column * acc_in[
+                    j, :, place * dim : (place + 1) * dim
+                ].astype(jnp.float32)
+            attn[me, :, place * dim : (place + 1) * dim] = joined.astype(jnp.bfloat16)
+
+        def attn_copy(d, source):
+            return send(
+                attn.at[source], attn.at[source], t_s.at[d], t_r.at[d], "gy", lax.rem(me + d, blocks)
+            )
+
+        for d in range(1, blocks):
+            attn_copy(d, me).start()
+        load.wait()
+
+        def project(source):
+            return jnp.dot(
+                attn[source],
+                wo[pl.ds(pl.multiple_of(source * width, width), width), :],
+                preferred_element_type=jnp.float32,
+            )
+
+        total = st_ref[...].astype(jnp.float32) + project(me)
+        for d in range(1, blocks):
+            source = lax.rem(me + blocks - d, blocks)
+            attn_copy(d, source).wait_recv()
+            total = total + project(source)
+        h_ref[row] = total.astype(jnp.bfloat16)
+
+        def h_copy(d, source):
+            return send(
+                h_ref.at[source], h_ref.at[source], h_s.at[d], h_r.at[d], "gx",
+                lax.rem(row + d, rows_gx),
+            )
+
+        for d in range(1, rows_gx):
+            h_copy(d, row).start()
+        for d in range(1, blocks):
+            block = lax.rem(me + d, blocks)
+            for copy in part_copies(block, me):
+                copy.wait_send()
+            attn_copy(d, me).wait_send()
+        for d in range(1, rows_gx):
+            h_copy(d, lax.rem(row + rows_gx - d, rows_gx)).wait_recv()
+            h_copy(d, row).wait_send()
+
+    vmem = pl.BlockSpec(memory_space=pltpu.VMEM)
+    dma = pltpu.SemaphoreType.DMA
     return pl.pallas_call(
         kernel,
-        grid=(kv_heads,),
         out_shape=[
-            jax.ShapeDtypeStruct((blocks, tokens, per_block * dim), jnp.bfloat16),
-            jax.ShapeDtypeStruct((blocks, 2 * per_block, 128), jnp.float32),
+            jax.ShapeDtypeStruct((rows_gx, tokens, cols), jnp.bfloat16),
             jax.ShapeDtypeStruct((tokens, kv_cols), jnp.bfloat16),
         ],
-        in_specs=[
-            pl.BlockSpec(memory_space=pltpu.SMEM),
-            pl.BlockSpec((tokens, group * dim), lambda g: (0, g)),
-            pl.BlockSpec((tokens, dim), lambda g: (0, heads + g)),
-            pl.BlockSpec((tokens, dim), lambda g: (0, heads + kv_heads + g)),
-            whole((1, dim)),
-            whole((1, dim)),
-            whole((tokens, dim)),
-            whole((tokens, dim)),
-            pl.BlockSpec((span, dim), lambda g: (0, g)),
-            pl.BlockSpec((span, dim), lambda g: (0, g)),
-            whole((tokens, tokens)),
+        in_specs=[pl.BlockSpec(memory_space=pltpu.SMEM)]
+        + [vmem] * 9
+        + [pl.BlockSpec(memory_space=pl.ANY)],
+        out_specs=[vmem, vmem],
+        scratch_shapes=[
+            pltpu.VMEM((blocks, tokens, width), jnp.bfloat16),
+            pltpu.VMEM((blocks, 2 * per_block, 128), jnp.float32),
+            pltpu.VMEM((blocks, tokens, width), jnp.bfloat16),
+            pltpu.VMEM((blocks, 2 * per_block, 128), jnp.float32),
+            pltpu.VMEM((blocks, tokens, width), jnp.bfloat16),
+            pltpu.VMEM(w_o.shape, jnp.bfloat16),
+            dma,
+            dma((blocks,)),
+            dma((blocks,)),
+            dma((blocks,)),
+            dma((blocks,)),
+            dma((blocks,)),
+            dma((blocks,)),
+            dma((rows_gx,)),
+            dma((rows_gx,)),
         ],
-        out_specs=[
-            pl.BlockSpec((blocks_here, tokens, per_block * dim), lambda g: (g, 0, 0)),
-            pl.BlockSpec((blocks_here, 2 * per_block, 128), lambda g: (g, 0, 0)),
-            pl.BlockSpec((tokens, dim), lambda g: (0, g)),
-        ],
-        compiler_params=pltpu.CompilerParams(vmem_limit_bytes=40 * 1024 * 1024),
-        name="attend",
-    )(bounds, qkv, qkv, qkv, q_gain, k_gain, cosine, sine, cache_k, cache_v, tree_mask)
+        compiler_params=pltpu.CompilerParams(
+            collective_id=cid, has_side_effects=True, vmem_limit_bytes=48 * 1024 * 1024
+        ),
+        name="attention_block",
+    )(
+        limit, qkv, q_gain, k_gain, cosine, sine, cache_k, cache_v, tree_mask, states_here, w_o
+    )
 
 
 def rms_scale(values, gain):
@@ -414,10 +547,8 @@
     q_cols = heads_all * head_dim
     depth = jnp.sum(tree_mask, -1) - 1
     cosine, sine = angles_of((cache_len[:, None] + depth)[0], head_dim)
-    bounds = jnp.concatenate([cache_len - col_index * cache_span, col_index[None]])
-    count_gy = lax.axis_size("gy")
-    heads_here = heads_all // count_gy
-    blocks, stats, k_rot = attend(
+    states_here = lax.dynamic_slice_in_dim(states, col_index * cols_here, cols_here, 1)
+    gathered, k_rot = attention_block(
         qkv_whole,
         q_gain[None],
         k_gain[None],
@@ -425,28 +556,13 @@
         sine,
         cache_k[0],
         cache_v[0],
-        bounds,
+        cache_len - col_index * cache_span,
         tree_mask[0],
-        count_gy,
+        states_here,
+        w_o,
+        1,
     )
-    blocks, stats = exchange([blocks, stats], "gy", True, 1)
-    stats = stats[:, :, :tok_rows].reshape(count_gy, 2, heads_here, tok_rows)
-    stats = jnp.swapaxes(stats, 2, 3)
-    factor = jnp.exp(stats[:, 0] - jnp.max(stats[:, 0], 0))
-    denom = jnp.sum(stats[:, 1] * factor, 0)
-    factor = factor / denom
-    attn_part = jnp.sum(
-        blocks.astype(jnp.float32).reshape(count_gy, tok_rows, heads_here, head_dim)
-        * factor[..., None],
-        0,
-    )
-    attn_part = attn_part.astype(jnp.bfloat16).reshape(tok_rows, heads_here * head_dim)
-    (attn,) = exchange([attn_part], "gy", False, 2)
-    attn = jnp.swapaxes(attn, 0, 1).reshape(tok_rows, q_cols)
-    states_here = lax.dynamic_slice_in_dim(states, col_index * cols_here, cols_here, 1)
-    resid = (
-        states_here.astype(jnp.float32) + jnp.dot(attn, w_o, preferred_element_type=jnp.float32)
-    ).astype(jnp.bfloat16)
+    resid = lax.dynamic_index_in_dim(gathered, row_index, 0, False)
     exp_here = w_in.shape[0]
     expert_count = exp_here * count_gx
     top_k = routing.shape[1]
@@ -472,7 +588,6 @@
     pick = slot_of.T[:, None, :] == jnp.arange(slots, dtype=jnp.int32)[None, :, None]
     pick_matrix = pick.astype(jnp.bfloat16)
     slot_weight = jnp.sum(jnp.where(pick, weights.T[:, None, :], 0.0), -1)
-    (gathered,) = exchange([resid], "gx", False, 3)
     gathered = gathered.reshape(tokens, cols_here).astype(jnp.float32)
     token_squares = jnp.sum(gathered * gathered, -1)
     slot_squares = jnp.sum(jnp.where(pick, token_squares, 0.0), -1)

time: 184 us -> 161 us (0.88)
  Pallas kernels: 150 us -> 138 us
  matrix products: 14.5 us -> 10.9 us
  local copies, waits for them, and re-layouts: 5.89 us -> 2.39 us
  other arithmetic: 11 us -> 7.98 us
    pallas_call x5 -> x2, Pallas kernels: 82.8 us -> 39.7 us  [exchange(): pl.pallas_call(kernel, out_shape=outs, in_specs=[pl.BlockSpec(memory_spac...]
    pallas_call x1, Pallas kernels: 9.55 us -> 38.9 us  [attention_block(): pl.pallas_call(kernel, out_shape=[jax.ShapeDtypeStruct((rows_gx, tokens,...]
    dot_general x1 -> x0, matrix products: 3.67 us -> none  [body(): jnp.dot(attn, w_o, preferred_element_type=jnp.float32)]
    unnamed x20 -> x12, local copies, waits for them, and re-layouts: 1.96 us -> 0.03 us
where the time goes in v3:
time: 161 us
  Pallas kernels  138 us (86%)
  matrix products  10.9 us (7%)
  other arithmetic  7.98 us (5%)
  local copies, waits for them, and re-layouts  2.39 us (1%)
    pallas_call x1, Pallas kernels, expert_hidden(): pl.pallas_call(kernel, out_shape=jax.ShapeDtypeStruct((2, chunks, piece,...  59.2 us
    pallas_call x2, Pallas kernels, exchange(): pl.pallas_call(kernel, out_shape=outs, in_specs=[pl.BlockSpec(memory_spac...  39.7 us
    pallas_call x1, Pallas kernels, attention_block(): pl.pallas_call(kernel, out_shape=[jax.ShapeDtypeStruct((rows_gx, tokens,...  38.9 us
    dot_general x1, matrix products, body(): jnp.einsum('est,esd->td', pick_matrix, expert_out, preferred_element_type...  5.14 us
    dot_general x1, matrix products, body(): jnp.dot(normed, w_qkv, preferred_element_type=jnp.float32)  4.32 us

profile of v3, /device:TPU:1, one launch (start us, length us, event | category | flops | bytes accessed | tf_op | source)
XLA Modules:
  0.0 160.6 jit_solution(6926985224210323787)
XLA Ops:
  1.3 0.9 reduce_sum.66
  2.2 1.1 fusion.12
  3.3 0.7 convert_element_type.86
  4.0 0.8 compare_reduce_fusion
  4.8 0.1 reshape.79
  4.9 0.7 convert_element_type.77
  5.6 0.8 fusion.19
  6.5 0.1 fusion.6
  6.6 0.1 copy.28
  6.6 0.1 reshape.80
  6.7 0.8 constant_dynamic-slice_fusion.st_ref
  7.6 0.2 fusion.27
  7.8 0.1 pad_maximum_fusion
  7.8 4.3 %convolution_convert_fusion.refs_0_ = bf16[64,1280]{1,0:T(8,128)(2,1)} fusion(bf16[2048,1280]{1,0:T(8,128)(2,1)} %param.18, bf16[64,2048]{1,0:T(8,128)(2,1)} %param.16, f32[2048]{0:T(1024)S(1)} %convert_element_type.77, f32[64]{0:T(128)S(1)} %add_rsqrt_fusion), kind=kOutput, calls=%fused_computation | convolution fusion | flops 336150528 | bytes 5677312 | tf_op jit(solution)/shard_map/dot_general | solution.py:544
  12.2 0.0 copy-start.4
  12.2 18.0 %exchange_0.1 = bf16[4,64,1280]{2,1,0:T(8,128)(2,1)} custom-call(bf16[64,1280]{1,0:T(8,128)(2,1)} %convolution_convert_fusion.refs_0_), custom_call_target="tpu_custom_call" | custom-call | tf_op jit(solution)/shard_map/exchange_0/pallas_call | solution.py:59
  30.2 1.1 copy.29
  31.4 0.0 copy-done
  31.4 0.0 copy-start.5
  31.4 38.9 %attention_block.1 = (bf16[8,64,512]{2,1,0:T(8,128)(2,1)S(1)}, bf16[64,512]{1,0:T(8,128)(2,1)S(1)}) custom-call(s32[1]{0:T(128)S(6)} %sub.11.limit_ref, bf16[64,5120]{1,0:T(8,128)(2,1)S(1)} %bitcast.50, bf16[1,128]{1,0:T(2,128)(2,1)S(1)} %bitcast.55, bf16[1,128]{1,0:T(2,128)(2,1)S(1)} %bitcast.56, f32[64,128]{1,0:T(8,128)S(1)} %get-tuple-element.11.cos_ref, ...), custom_call_target="tpu_custom_call" | custom-call | tf_op jit(solution)/shard_map/attention_block/pallas_call | solution.py:466
  70.4 0.7 fusion.7
  71.1 0.2 multiply_reduce_fusion
  71.3 0.1 reduce_sum.68
  71.4 0.6 select_reduce_fusion
  72.0 0.1 reshape.81
  72.0 0.1 fusion.8
  72.1 0.6 fusion.2.x_ref
  72.7 59.2 %expert_hidden.1 = bf16[2,24,16,768]{3,2,1,0:T(8,128)(2,1)S(1)} custom-call(bf16[8,96,512]{2,1,0:T(8,128)(2,1)S(1)} %fusion.2.x_ref, f32[48,128]{1,0:T(8,128)S(1)} %pad.4.sq_ref, bf16[8,512,1536]{2,1,0:T(8,128)(2,1)} %w_hbm.1), custom_call_target="tpu_custom_call" | custom-call | tf_op jit(solution)/shard_map/expert_hidden/pallas_call | solution.py:241
  132.0 5.1 %fusion.4 = bf16[512,512]{1,0:T(8,128)(2,1)} fusion(bf16[8,96,768]{2,1,0:T(8,128)(2,1)S(1)} %bitcast.51, bf16[8,768,512]{2,1,0:T(8,128)(2,1)} %param.30, f32[8,96]{1,0:T(8,128)S(1)} %get-tuple-element.6, s32[8,512]{1,0:T(8,128)S(1)} %select_bitcast_fusion), kind=kOutput, calls=%fused_computation.9 | convolution fusion | flops 1008074752 | bytes 8014848 | tf_op jit(solution)/shard_map/est,esd->td/dot_general | solution.py:603
  137.1 21.7 %exchange_5.1 = bf16[8,64,512]{2,1,0:T(8,128)(2,1)} custom-call(bf16[8,64,512]{2,1,0:T(8,128)(2,1)} %bitcast.58), custom_call_target="tpu_custom_call" | custom-call | tf_op jit(solution)/shard_map/exchange_5/pallas_call | solution.py:59
  158.8 1.1 convert_reduce_fusion
  160.0 0.7 fusion.23
  (17 shorter events, 0.1 us)
Async XLA Ops:
  12.2 19.2 %copy-start = (bf16[1,1024,512]{2,1,0:T(8,128)(2,1)S(1)}, bf16[1,1024,512]{2,1,0:T(8,128)(2,1)}, u32[]{:S(2)}) copy-start(bf16[1,1024,512]{2,1,0:T(8,128)(2,1)} %param.21) | copy-start | bytes 3145732
  12.2 19.2 %copy-start.1 = (bf16[1,1024,512]{2,1,0:T(8,128)(2,1)S(1)}, bf16[1,1024,512]{2,1,0:T(8,128)(2,1)}, u32[]{:S(2)}) copy-start(bf16[1,1024,512]{2,1,0:T(8,128)(2,1)} %param.22) | copy-start | bytes 3145732
  12.2 19.2 %copy-start.2 = (s32[1,64,64]{2,1,0:T(8,128)S(1)}, s32[1,64,64]{2,1,0:T(8,128)}, u32[]{:S(2)}) copy-start(s32[1,64,64]{2,1,0:T(8,128)} %param.24) | copy-start | bytes 49156
  12.2 19.2 %copy-start.3 = (bf16[128]{0:T(256)(128)(2,1)S(1)}, bf16[128]{0:T(256)(128)(2,1)}, u32[]{:S(2)}) copy-start(bf16[128]{0:T(256)(128)(2,1)} %param.19) | copy-start | bytes 772
  12.2 19.2 %copy-start.4 = (bf16[128]{0:T(256)(128)(2,1)S(1)}, bf16[128]{0:T(256)(128)(2,1)}, u32[]{:S(2)}) copy-start(bf16[128]{0:T(256)(128)(2,1)} %param.20) | copy-start | bytes 772
  31.4 38.9 %copy-start.5 = (s32[1,8,64]{2,1,0:T(8,128)S(1)}, s32[1,8,64]{2,1,0:T(8,128)}, u32[]{:S(2)}) copy-start(s32[1,8,64]{2,1,0:T(8,128)} %param.31) | copy-start | bytes 6148

commit v4 on v3

--- a/solution.py
+++ b/solution.py
@@ -71,10 +71,12 @@
     )(*arrays)
 
 
-def expert_hidden(rows, squares, w_in, model_width, cid):
+def expert_layer(rows, squares, w_in, w_down, slot_weight, pick_back, resid, model_width, cid):
     axis = "gy"
     count = lax.axis_size(axis)
+    peers = lax.axis_size("gx")
     experts, slots, depth = rows.shape
+    tokens, cols = resid.shape
     wide = w_in.shape[2]
     units = wide // 2
     half = experts // 2
@@ -85,8 +87,9 @@
     far = hop * (count - 1)
 
     def kernel(
-        x_ref, sq_ref, w_hbm, hid_ref, wbuf, part, rbuf, sqbuf, inv_ref,
-        wsem, rs_s, rs_r, h_s, h_r, sq_s, sq_r,
+        x_ref, sq_ref, weight_ref, pick_ref, resid_ref, w_hbm, d_hbm, out_ref,
+        hid_ref, wbuf, dbuf, part, rbuf, sqbuf, inv_ref, obuf, pbuf, ret,
+        wsem, dsem, rs_s, rs_r, h_s, h_r, sq_s, sq_r, g_s, g_r,
     ):
         me = lax.axis_index(axis)
         prev = lax.rem(me + count - 1, count)
@@ -97,15 +100,36 @@
         def load(e):
             return pltpu.make_async_copy(w_hbm.at[e], wbuf.at[e], wsem.at[e])
 
+        def load_down(e):
+            return pltpu.make_async_copy(d_hbm.at[e], dbuf.at[e], dsem.at[e])
+
+        row = lax.axis_index("gx")
         for s in range(half):
             load(half + s).start()
             load(s).start()
+        for s in range(half):
+            load_down(half + s).start()
+            load_down(s).start()
         barrier = pltpu.get_barrier_semaphore()
         for d in range(1, count):
             pl.semaphore_signal(
                 barrier, inc=1, device_id={axis: lax.rem(me + d, count)}, device_id_type=MESH
             )
-        pl.semaphore_wait(barrier, count - 1)
+        for d in range(1, peers):
+            pl.semaphore_signal(
+                barrier, inc=1, device_id={"gx": lax.rem(row + d, peers)}, device_id_type=MESH
+            )
+
+        def multiply(h, s):
+            e = h * half + s
+            load(e).wait()
+            value = jnp.dot(x_ref[e], wbuf[e], preferred_element_type=jnp.float32)
+            for j in range(sub):
+                part[h, s * sub + j] = value[j * piece : (j + 1) * piece].astype(jnp.bfloat16)
+
+        multiply(1, 0)
+        multiply(0, 0)
+        pl.semaphore_wait(barrier, count + peers - 2)
 
         def sq_copy(d):
             return pltpu.make_async_remote_copy(
@@ -119,11 +143,14 @@
 
         for d in range(1, count):
             sq_copy(d).start()
-        total = sq_ref[...]
-        for d in range(1, count):
-            sq_copy(d).wait()
-            total = total + sqbuf[d]
-        inv_ref[...] = lax.rsqrt(total / model_width + EPS)
+
+        def finish_squares():
+            total = sq_ref[...]
+            for d in range(1, count):
+                sq_copy(d).wait()
+                total = total + sqbuf[d]
+            inv_ref[...] = lax.rsqrt(total / model_width + EPS)
+
         diagonal = lax.broadcasted_iota(jnp.int32, (piece, 128), 0) == lax.broadcasted_iota(
             jnp.int32, (piece, 128), 1
         )
@@ -189,18 +216,23 @@
             def _():
                 hid_copy(h, c).start()
 
-        def multiply(s):
-            for h in (1, 0):
-                e = h * half + s
-                load(e).wait()
-                value = jnp.dot(x_ref[e], wbuf[e], preferred_element_type=jnp.float32)
-                for j in range(sub):
-                    part[h, s * sub + j] = value[j * piece : (j + 1) * piece].astype(jnp.bfloat16)
+        def project(h, s):
+            e = h * half + s
+            load_down(e).wait()
+            value = hid_ref[h, pl.ds(s * sub, sub)].reshape(slots, units)
+            value = jnp.dot(value, dbuf[e], preferred_element_type=jnp.float32)
+            obuf[e] = (value * weight_ref[e]).astype(jnp.bfloat16)
 
         def step(t, carry):
-            @pl.when(jnp.logical_and(t < chunks, lax.rem(t, sub) == 0))
+            for h, place in ((1, 1), (0, sub // 2 + 1)):
+
+                @pl.when(jnp.logical_and(t < chunks - sub, lax.rem(t, sub) == place))
+                def _():
+                    multiply(h, lax.div(t, sub) + 1)
+
+            @pl.when(t == far - 1)
             def _():
-                multiply(lax.div(t, sub))
+                finish_squares()
 
             for h in (1, 0):
                 way = hop * (me if h else count - 1 - me)
@@ -218,6 +250,10 @@
                 def _():
                     return_chunk(h, b)
 
+                    @pl.when(lax.rem(b, sub) == sub - 1)
+                    def _():
+                        project(h, lax.div(b, sub))
+
             return carry
 
         lax.fori_loop(0, chunks + 2 * far, step, 0)
@@ -236,37 +272,71 @@
 
             return carry
 
+        summed = jnp.dot(
+            pick_ref[...],
+            obuf[...].reshape(experts * slots, cols),
+            preferred_element_type=jnp.float32,
+        )
+        for p in range(peers):
+            pbuf[p] = summed[p * tokens : (p + 1) * tokens].astype(jnp.bfloat16)
+
+        def back_copy(d):
+            peer = lax.rem(row + d, peers)
+            return pltpu.make_async_remote_copy(
+                src_ref=pbuf.at[peer],
+                dst_ref=ret.at[d],
+                send_sem=g_s.at[d],
+                recv_sem=g_r.at[d],
+                device_id={"gx": peer},
+                device_id_type=MESH,
+            )
+
+        for d in range(1, peers):
+            back_copy(d).start()
+        moe = pbuf[row].astype(jnp.float32)
         lax.fori_loop(0, chunks, finish, 0)
-
-    hidden = pl.pallas_call(
+        for d in range(1, peers):
+            back_copy(d).wait_recv()
+            moe = moe + ret[d].astype(jnp.float32)
+        out_ref[...] = (resid_ref[...].astype(jnp.float32) + moe).astype(jnp.bfloat16)
+        for d in range(1, peers):
+            back_copy(d).wait_send()
+
+    vmem = pl.BlockSpec(memory_space=pltpu.VMEM)
+    hbm = pl.BlockSpec(memory_space=pl.ANY)
+    dma = pltpu.SemaphoreType.DMA
+    return pl.pallas_call(
         kernel,
-        out_shape=jax.ShapeDtypeStruct((2, chunks, piece, units), jnp.bfloat16),
-        in_specs=[
-            pl.BlockSpec(memory_space=pltpu.VMEM),
-            pl.BlockSpec(memory_space=pltpu.VMEM),
-            pl.BlockSpec(memory_space=pl.ANY),
-        ],
-        out_specs=pl.BlockSpec(memory_space=pltpu.VMEM),
+        out_shape=jax.ShapeDtypeStruct((tokens, cols), jnp.bfloat16),
+        in_specs=[vmem] * 5 + [hbm, hbm],
+        out_specs=vmem,
         scratch_shapes=[
+            pltpu.VMEM((2, chunks, piece, units), jnp.bfloat16),
             pltpu.VMEM((experts, depth, wide), jnp.bfloat16),
+            pltpu.VMEM((experts, units, cols), jnp.bfloat16),
             pltpu.VMEM((2, chunks, piece, wide), jnp.bfloat16),
             pltpu.VMEM((2, chunks, piece, wide), jnp.bfloat16),
             pltpu.VMEM((count, 2 * chunks, 128), jnp.float32),
             pltpu.VMEM((2 * chunks, 128), jnp.float32),
-            pltpu.SemaphoreType.DMA((experts,)),
-            pltpu.SemaphoreType.DMA((2, chunks)),
-            pltpu.SemaphoreType.DMA((2, chunks)),
-            pltpu.SemaphoreType.DMA((2, chunks)),
-            pltpu.SemaphoreType.DMA((2, chunks)),
-            pltpu.SemaphoreType.DMA((count,)),
-            pltpu.SemaphoreType.DMA((count,)),
+            pltpu.VMEM((experts, slots, cols), jnp.bfloat16),
+            pltpu.VMEM((peers, tokens, cols), jnp.bfloat16),
+            pltpu.VMEM((peers, tokens, cols), jnp.bfloat16),
+            dma((experts,)),
+            dma((experts,)),
+            dma((2, chunks)),
+            dma((2, chunks)),
+            dma((2, chunks)),
+            dma((2, chunks)),
+            dma((count,)),
+            dma((count,)),
+            dma((peers,)),
+            dma((peers,)),
         ],
         compiler_params=pltpu.CompilerParams(
-            collective_id=cid, has_side_effects=True, vmem_limit_bytes=48 * 1024 * 1024
+            collective_id=cid, has_side_effects=True, vmem_limit_bytes=52 * 1024 * 1024
         ),
-        name="expert_hidden",
-    )(rows, squares, w_in)
-    return hidden.reshape(experts, slots, units)
+        name="expert_layer",
+    )(rows, squares, slot_weight, pick_back, resid, w_in, w_down)
 
 
 def attention_block(
@@ -597,17 +667,17 @@
     rows = jnp.einsum(
         "est,td->esd", pick_matrix, scaled, preferred_element_type=jnp.float32
     ).astype(jnp.bfloat16)
-    hidden = expert_hidden(rows, slot_squares, w_in, model_width, 4)
-    expert_out = jnp.einsum("esf,efd->esd", hidden, w_down, preferred_element_type=jnp.float32)
-    expert_out = (expert_out * slot_weight[..., None]).astype(jnp.bfloat16)
-    partial_moe = jnp.einsum(
-        "est,esd->td", pick_matrix, expert_out, preferred_element_type=jnp.float32
-    ).astype(jnp.bfloat16)
-    (returned,) = exchange(
-        [partial_moe.reshape(count_gx, tok_rows, cols_here)], "gx", True, 5
+    layer_out = expert_layer(
+        rows,
+        slot_squares,
+        w_in,
+        w_down,
+        slot_weight[..., None],
+        pick_matrix.reshape(exp_here * slots, tokens).T,
+        resid,
+        model_width,
+        4,
     )
-    moe_total = jnp.sum(returned.astype(jnp.float32), 0)
-    layer_out = (resid.astype(jnp.float32) + moe_total).astype(jnp.bfloat16)
     kv_new = jnp.concatenate([k_rot, qkv_whole[:, q_cols + kv_cols :]], -1)[None]
     accepted_kv = jnp.einsum(
         "rat,rtc->rac", accept.astype(jnp.bfloat16), kv_new, preferred_element_type=jnp.float32

time: 161 us -> 153 us (0.950)
  Pallas kernels: 138 us -> 131 us
  matrix products: 10.9 us -> 5.72 us
  local copies, waits for them, and re-layouts: 2.39 us -> 6.53 us
    pallas_call x2 -> x1, Pallas kernels: 39.7 us -> 18 us  [exchange(): pl.pallas_call(kernel, out_shape=outs, in_specs=[pl.BlockSpec(memory_spac...]
    pallas_call x1, Pallas kernels: 59.2 us -> 74 us  [expert_layer(): pl.pallas_call(kernel, out_shape=jax.ShapeDtypeStruct((tokens, cols), jnp...]
    dot_general x1 -> x0, matrix products: 5.14 us -> none  [body(): jnp.einsum('est,esd->td', pick_matrix, expert_out, preferred_element_type...]
    eq x0 -> x4, local copies, waits for them, and re-layouts: none -> 3.3 us  [body(): slot_of.T[:, None, :] == jnp.arange(slots, dtype=jnp.int32)[None, :, None]]
where the time goes in v4:
time: 153 us; the launch traced here: 152 us
  Pallas kernels  131 us (86%)
  other arithmetic  7.2 us (5%)
  local copies, waits for them, and re-layouts  6.53 us (4%)
  matrix products  5.72 us (4%)
    pallas_call x1, Pallas kernels, expert_layer(): pl.pallas_call(kernel, out_shape=jax.ShapeDtypeStruct((tokens, cols), jnp...  74 us
    pallas_call x1, Pallas kernels, attention_block(): pl.pallas_call(kernel, out_shape=[jax.ShapeDtypeStruct((rows_gx, tokens,...  39 us
    pallas_call x1, Pallas kernels, exchange(): pl.pallas_call(kernel, out_shape=outs, in_specs=[pl.BlockSpec(memory_spac...  18 us
    dot_general x1, matrix products, body(): jnp.dot(normed, w_qkv, preferred_element_type=jnp.float32)  4.31 us
    eq x4, local copies, waits for them, and re-layouts, body(): slot_of.T[:, None, :] == jnp.arange(slots, dtype=jnp.int32)[None, :, None]  3.3 us

profile of v4, /device:TPU:1, one launch (start us, length us, event | category | flops | bytes accessed | tf_op | source)
XLA Modules:
  0.0 152.0 jit_solution(14588761596341570798)
XLA Ops:
  1.3 0.9 reduce_sum.57
  2.2 1.1 fusion.8
  3.3 0.7 convert_element_type.67
  4.0 0.8 compare_reduce_fusion
  4.9 0.1 eq.45
  4.9 0.1 reshape.72
  5.0 0.7 convert_element_type.61
  5.7 0.8 fusion.15
  6.6 0.1 fusion.3
  6.6 0.1 copy.30
  6.7 0.1 reshape.73
  6.8 0.8 constant_dynamic-slice_fusion.st_ref
  7.6 0.2 fusion.22
  7.8 0.1 pad_maximum_fusion
  7.9 4.3 %convolution_convert_fusion.refs_0_ = bf16[64,1280]{1,0:T(8,128)(2,1)} fusion(bf16[2048,1280]{1,0:T(8,128)(2,1)} %param.18, bf16[64,2048]{1,0:T(8,128)(2,1)} %param.16, f32[2048]{0:T(1024)S(1)} %convert_element_type.61, f32[64]{0:T(128)S(1)} %add_rsqrt_fusion), kind=kOutput, calls=%fused_computation | convolution fusion | flops 336150528 | bytes 5677312 | tf_op jit(solution)/shard_map/dot_general | solution.py:614
  12.3 0.0 copy-start.4
  12.3 18.0 %exchange_0.1 = bf16[4,64,1280]{2,1,0:T(8,128)(2,1)} custom-call(bf16[64,1280]{1,0:T(8,128)(2,1)} %convolution_convert_fusion.refs_0_), custom_call_target="tpu_custom_call" | custom-call | tf_op jit(solution)/shard_map/exchange_0/pallas_call | solution.py:59
  30.3 1.1 copy.34
  31.5 39.0 %attention_block.1 = (bf16[8,64,512]{2,1,0:T(8,128)(2,1)S(1)}, bf16[64,512]{1,0:T(8,128)(2,1)S(1)}) custom-call(s32[1]{0:T(128)S(6)} %sub.11.limit_ref, bf16[64,5120]{1,0:T(8,128)(2,1)S(1)} %bitcast.45, bf16[1,128]{1,0:T(2,128)(2,1)S(1)} %bitcast.49, bf16[1,128]{1,0:T(2,128)(2,1)S(1)} %bitcast.50, f32[64,128]{1,0:T(8,128)S(1)} %get-tuple-element.11.cos_ref, ...), custom_call_target="tpu_custom_call" | custom-call | tf_op jit(solution)/shard_map/attention_block/pallas_call | solution.py:536
  70.6 0.7 fusion.4
  71.3 0.2 multiply_reduce_fusion
  71.5 0.1 reduce_sum.59
  71.6 0.6 select_reduce_fusion
  72.1 0.1 reshape.75
  72.3 0.1 fusion.5
  72.4 0.6 fusion.1.x_ref
  72.9 0.2 copy.33.weight_ref
  73.1 1.4 eq.40
  74.5 1.9 %copy.32 = s32[768,512]{0,1:T(8,128)S(1)} copy(s32[768,512]{1,0:T(8,128)} %bitcast.51) | data formatting | bytes 3145728 | tf_op jit(solution)/shard_map/eq | solution.py:658
  76.4 1.0 fusion.6.pick_ref
  77.4 74.0 %expert_layer.1 = bf16[64,512]{1,0:T(8,128)(2,1)S(1)} custom-call(bf16[8,96,512]{2,1,0:T(8,128)(2,1)S(1)} %fusion.1.x_ref, f32[48,128]{1,0:T(8,128)S(1)} %pad.4.sq_ref, f32[8,96,1]{2,1,0:T(8,128)S(1)} %copy.33.weight_ref, bf16[512,768]{1,0:T(8,128)(2,1)} %fusion.6.pick_ref, bf16[64,512]{1,0:T(8,128)(2,1)S(1)} %dynamic-slice_bitcast_fusion.resid_ref, ...), custom_call_target="tpu_custom_call" | custom-call | tf_op jit(solution)/shard_map/expert_layer/pallas_call | solution.py:308
  151.4 0.6 copy.39
  (21 shorter events, 0.1 us)
Async XLA Ops:
  12.2 19.2 %copy-start = (bf16[1,1024,512]{2,1,0:T(8,128)(2,1)S(1)}, bf16[1,1024,512]{2,1,0:T(8,128)(2,1)}, u32[]{:S(2)}) copy-start(bf16[1,1024,512]{2,1,0:T(8,128)(2,1)} %param.21) | copy-start | bytes 3145732
  12.3 19.2 %copy-start.1 = (bf16[1,1024,512]{2,1,0:T(8,128)(2,1)S(1)}, bf16[1,1024,512]{2,1,0:T(8,128)(2,1)}, u32[]{:S(2)}) copy-start(bf16[1,1024,512]{2,1,0:T(8,128)(2,1)} %param.22) | copy-start | bytes 3145732
  12.3 19.2 %copy-start.2 = (s32[1,64,64]{2,1,0:T(8,128)S(1)}, s32[1,64,64]{2,1,0:T(8,128)}, u32[]{:S(2)}) copy-start(s32[1,64,64]{2,1,0:T(8,128)} %param.24) | copy-start | bytes 49156
  12.3 19.2 %copy-start.3 = (bf16[128]{0:T(256)(128)(2,1)S(1)}, bf16[128]{0:T(256)(128)(2,1)}, u32[]{:S(2)}) copy-start(bf16[128]{0:T(256)(128)(2,1)} %param.19) | copy-start | bytes 772
  12.3 19.2 %copy-start.4 = (bf16[128]{0:T(256)(128)(2,1)S(1)}, bf16[128]{0:T(256)(128)(2,1)}, u32[]{:S(2)}) copy-start(bf16[128]{0:T(256)(128)(2,1)} %param.20) | copy-start | bytes 772
  31.5 39.0 %copy-start.5 = (s32[1,8,64]{2,1,0:T(8,128)S(1)}, s32[1,8,64]{2,1,0:T(8,128)}, u32[]{:S(2)}) copy-start(s32[1,8,64]{2,1,0:T(8,128)} %param.31) | copy-start | bytes 6148

commit v5 on v4

--- a/solution.py
+++ b/solution.py
@@ -272,9 +272,10 @@
 
             return carry
 
-        summed = jnp.dot(
+        summed = lax.dot_general(
             pick_ref[...],
             obuf[...].reshape(experts * slots, cols),
+            (((0,), (0,)), ((), ())),
             preferred_element_type=jnp.float32,
         )
         for p in range(peers):
@@ -673,7 +674,7 @@
         w_in,
         w_down,
         slot_weight[..., None],
-        pick_matrix.reshape(exp_here * slots, tokens).T,
+        pick_matrix.reshape(exp_here * slots, tokens),
         resid,
         model_width,
         4,

time: 153 us -> 150 us (0.980)
  local copies, waits for them, and re-layouts: 6.53 us -> 3.3 us
    eq x4 -> x2, local copies, waits for them, and re-layouts: 3.3 us -> 0.08 us  [body(): slot_of.T[:, None, :] == jnp.arange(slots, dtype=jnp.int32)[None, :, None]]
where the time goes in v5:
time: 150 us; the launch traced here: 149 us
  Pallas kernels  131 us (87%)
  other arithmetic  7.27 us (5%)
  matrix products  5.72 us (4%)
  local copies, waits for them, and re-layouts  3.3 us (2%)
  between operations  1.52 us (1%)
    pallas_call x1, Pallas kernels, expert_layer(): pl.pallas_call(kernel, out_shape=jax.ShapeDtypeStruct((tokens, cols), jnp...  74.2 us
    pallas_call x1, Pallas kernels, attention_block(): pl.pallas_call(kernel, out_shape=[jax.ShapeDtypeStruct((rows_gx, tokens,...  39 us
    pallas_call x1, Pallas kernels, exchange(): pl.pallas_call(kernel, out_shape=outs, in_specs=[pl.BlockSpec(memory_spac...  18 us
    dot_general x1, matrix products, body(): jnp.dot(normed, w_qkv, preferred_element_type=jnp.float32)  4.31 us

profile of v5, /device:TPU:1, one launch (start us, length us, event | category | flops | bytes accessed | tf_op | source)
XLA Modules:
  0.0 149.0 jit_solution(1141997004699449046)
XLA Ops:
  1.3 0.9 reduce_sum.57
  2.2 1.1 fusion.8
  3.3 0.7 convert_element_type.69
  4.0 0.8 compare_reduce_fusion
  4.9 0.1 eq.45
  4.9 0.1 reshape.72
  5.0 0.7 convert_element_type.63
  5.7 0.8 fusion.15
  6.6 0.1 fusion.4
  6.6 0.1 copy.28
  6.7 0.1 reshape.73
  6.8 0.8 constant_dynamic-slice_fusion.st_ref
  7.6 0.2 fusion.22
  7.8 0.1 pad_maximum_fusion
  7.9 4.3 %convolution_convert_fusion.refs_0_ = bf16[64,1280]{1,0:T(8,128)(2,1)} fusion(bf16[2048,1280]{1,0:T(8,128)(2,1)} %param.18, bf16[64,2048]{1,0:T(8,128)(2,1)} %param.16, f32[2048]{0:T(1024)S(1)} %convert_element_type.63, f32[64]{0:T(128)S(1)} %add_rsqrt_fusion), kind=kOutput, calls=%fused_computation | convolution fusion | flops 336150528 | bytes 5677312 | tf_op jit(solution)/shard_map/dot_general | solution.py:615
  12.3 0.0 copy-start.4
  12.3 18.0 %exchange_0.1 = bf16[4,64,1280]{2,1,0:T(8,128)(2,1)} custom-call(bf16[64,1280]{1,0:T(8,128)(2,1)} %convolution_convert_fusion.refs_0_), custom_call_target="tpu_custom_call" | custom-call | tf_op jit(solution)/shard_map/exchange_0/pallas_call | solution.py:59
  30.3 1.1 copy.31
  31.5 0.0 copy-done
  31.5 0.0 copy-start.5
  31.5 39.0 %attention_block.1 = (bf16[8,64,512]{2,1,0:T(8,128)(2,1)S(1)}, bf16[64,512]{1,0:T(8,128)(2,1)S(1)}) custom-call(s32[1]{0:T(128)S(6)} %sub.11.limit_ref, bf16[64,5120]{1,0:T(8,128)(2,1)S(1)} %bitcast.46, bf16[1,128]{1,0:T(2,128)(2,1)S(1)} %bitcast.50, bf16[1,128]{1,0:T(2,128)(2,1)S(1)} %bitcast.51, f32[64,128]{1,0:T(8,128)S(1)} %get-tuple-element.11.cos_ref, ...), custom_call_target="tpu_custom_call" | custom-call | tf_op jit(solution)/shard_map/attention_block/pallas_call | solution.py:537
  70.6 0.7 fusion.5
  71.3 0.2 multiply_reduce_fusion
  71.5 0.1 reduce_sum.59
  71.6 0.6 select_reduce_fusion
  72.1 0.1 reshape.75
  72.3 0.1 fusion.6
  72.4 0.6 fusion.2.x_ref
  72.9 0.2 copy.30.weight_ref
  73.1 1.1 fusion.1.pick_ref
  74.2 74.2 %expert_layer.1 = bf16[64,512]{1,0:T(8,128)(2,1)S(1)} custom-call(bf16[8,96,512]{2,1,0:T(8,128)(2,1)S(1)} %fusion.2.x_ref, f32[48,128]{1,0:T(8,128)S(1)} %pad.4.sq_ref, f32[8,96,1]{2,1,0:T(8,128)S(1)} %copy.30.weight_ref, bf16[768,512]{1,0:T(8,128)(2,1)} %fusion.1.pick_ref, bf16[64,512]{1,0:T(8,128)(2,1)S(1)} %dynamic-slice_bitcast_fusion.resid_ref, ...), custom_call_target="tpu_custom_call" | custom-call | tf_op jit(solution)/shard_map/expert_layer/pallas_call | solution.py:309
  148.4 0.6 copy.36
  (19 shorter events, 0.1 us)
Async XLA Ops:
  12.2 19.2 %copy-start = (bf16[1,1024,512]{2,1,0:T(8,128)(2,1)S(1)}, bf16[1,1024,512]{2,1,0:T(8,128)(2,1)}, u32[]{:S(2)}) copy-start(bf16[1,1024,512]{2,1,0:T(8,128)(2,1)} %param.21) | copy-start | bytes 3145732
  12.3 19.2 %copy-start.1 = (bf16[1,1024,512]{2,1,0:T(8,128)(2,1)S(1)}, bf16[1,1024,512]{2,1,0:T(8,128)(2,1)}, u32[]{:S(2)}) copy-start(bf16[1,1024,512]{2,1,0:T(8,128)(2,1)} %param.22) | copy-start | bytes 3145732
  12.3 19.2 %copy-start.2 = (s32[1,64,64]{2,1,0:T(8,128)S(1)}, s32[1,64,64]{2,1,0:T(8,128)}, u32[]{:S(2)}) copy-start(s32[1,64,64]{2,1,0:T(8,128)} %param.24) | copy-start | bytes 49156
  12.3 19.2 %copy-start.3 = (bf16[128]{0:T(256)(128)(2,1)S(1)}, bf16[128]{0:T(256)(128)(2,1)}, u32[]{:S(2)}) copy-start(bf16[128]{0:T(256)(128)(2,1)} %param.19) | copy-start | bytes 772
  12.3 19.2 %copy-start.4 = (bf16[128]{0:T(256)(128)(2,1)S(1)}, bf16[128]{0:T(256)(128)(2,1)}, u32[]{:S(2)}) copy-start(bf16[128]{0:T(256)(128)(2,1)} %param.20) | copy-start | bytes 772
  31.5 39.0 %copy-start.5 = (s32[1,8,64]{2,1,0:T(8,128)S(1)}, s32[1,8,64]{2,1,0:T(8,128)}, u32[]{:S(2)}) copy-start(s32[1,8,64]{2,1,0:T(8,128)} %param.31) | copy-start | bytes 6148
